TPU v7x, 768 devices: a whole 4x8x12 slice. The times are simulated.
768 devices in a mesh: gx: 8 (over y), gy: 16 (over z_lo, x), gz: 6 (over z_hi, core).
Axes of the slice: x: 4, y: 8, z: 12 (z_hi: 3, z_lo: 4; z = z_hi * 4 + z_lo), core: 2. Of those that a mesh axis runs over, the one named last changes fastest.
Arguments:
- positions: float32 [16, 32, 6, 192], P('gx', 'gy', 'gz'), may hold values from 0 to 1
- species: int32 [16, 32, 6, 64], P('gx', 'gy', 'gz'), may hold values from 0 to 88
- counts: int32 [16, 32, 6], P('gx', 'gy', 'gz'), may hold values from 1 to 64, as said below
- embed: bfloat16 [89, 128], replicated, may hold values from -6 to 6
- filters: bfloat16 [128, 512], replicated, may hold values from -0.5 to 0.5
- w_up: bfloat16 [128, 128], replicated, may hold values from -0.5 to 0.5
- w_energy: float32 [128], replicated, may hold values from -0.5 to 0.5
Outputs:
- energies: float32 [16, 32, 6, 64], P('gx', 'gy', 'gz')
- forces: float32 [16, 32, 6, 192], P('gx', 'gy', 'gz')
Inputs may be any that keep to these rules, and one draw needn't show every extreme that they name: `counts`: at most 64 atoms a cell; some cell holds exactly 64 and some exactly 1.
All inputs are finite; a program needn't handle non-finite values.
Results may differ from a plain program's by a relative error of at most 0.0038.
Values may be sent and summed in bfloat16 or wider, within the bound.
A program may use at most 32 MiB of HBM per device.

v0:
```python
import jax
import jax.numpy as jnp
from jax import lax
from jax.sharding import PartitionSpec as P

MSG_SCALE = 0.1


def with_halo(block, sides, width):
    for axis, dim in sides:
        count = lax.axis_size(axis)
        forward = [(i, i + 1) for i in range(count - 1)]
        forward.append((count - 1, 0))
        backward = [(target, source) for source, target in forward]
        low = lax.ppermute(
            lax.slice_in_dim(block, block.shape[dim] - width, None, axis=dim), axis, forward
        )
        high = lax.ppermute(lax.slice_in_dim(block, 0, width, axis=dim), axis, backward)
        block = jnp.concatenate([low, block, high], axis=dim)
    return block


def radial(dist_sq, radial_count):
    decay_rates = 0.5 * 3.0 ** jnp.arange(radial_count).astype(jnp.float32)
    falloff = jnp.maximum(1.0 - dist_sq, 0.0)[..., None]
    decaying = jnp.exp(-decay_rates * dist_sq[..., None])
    return (
        decaying * falloff * falloff,
        -decaying * (decay_rates * falloff * falloff + 2.0 * falloff),
    )


def offset_of(index):
    first = index // 9 - 1
    second = index // 3 % 3 - 1
    third = index % 3 - 1
    return (first.astype(jnp.int32), second.astype(jnp.int32), third.astype(jnp.int32))


def geometry(anchor_pos, target_pos, offset):
    slot_count = anchor_pos.shape[-1] // 3
    leading = anchor_pos.shape[:-1]
    anchor = anchor_pos.reshape(leading + (3, slot_count))
    target = target_pos.reshape(leading + (3, slot_count))
    shift_vec = jnp.stack(offset).astype(jnp.float32).reshape((3, 1, 1))
    displace = target[..., :, None, :] - anchor[..., :, :, None] + shift_vec
    return (displace, jnp.sum(displace * displace, axis=-3))


def window(padded, offset, cell_shape):
    zero = jnp.zeros((), jnp.int32)
    starts = (offset[0] + 1, offset[1] + 1, offset[2] + 1) + (zero,) * (padded.ndim - 3)
    return lax.dynamic_slice(padded, starts, tuple(cell_shape) + padded.shape[3:])


def project(embedded, filters):
    return jnp.einsum(
        "abcsd,de->abcse", embedded, filters, preferred_element_type=jnp.float32
    ).astype(jnp.bfloat16)


def lookup(marked, embed):
    onehot = (marked[..., None] == jnp.arange(embed.shape[0], dtype=jnp.int32)).astype(jnp.bfloat16)
    return jnp.einsum("abcsk,kd->abcsd", onehot, embed, preferred_element_type=jnp.float32).astype(
        jnp.bfloat16
    )


def on_device(positions, species, counts, embed, filters, w_up, w_energy):
    cell_shape = positions.shape[:3]
    slot_count = species.shape[-1]
    feature_width = embed.shape[1]
    radial_count = filters.shape[1] // feature_width
    grouped_shape = cell_shape + (slot_count * radial_count, feature_width)
    centre = (jnp.zeros((), jnp.int32),) * 3
    occupied = (jnp.arange(slot_count, dtype=jnp.int32) < counts[..., None]).astype(jnp.float32)
    marked = jnp.where(occupied > 0.0, species, -1)
    pos_pad = with_halo(positions, (("gx", 0), ("gy", 1), ("gz", 2)), 1)
    embedded = lookup(marked, embed)
    feat_pad = with_halo(project(embedded, filters), (("gx", 0), ("gy", 1), ("gz", 2)), 1)
    anchor_feat = window(feat_pad, centre, cell_shape).reshape(grouped_shape)
    diagonal = jnp.eye(slot_count, dtype=jnp.float32)[..., None]

    def message_step(index, message):
        offset = offset_of(index)
        target_pos = window(pos_pad, offset, cell_shape)
        target_feat = window(feat_pad, offset, cell_shape).reshape(grouped_shape)
        displace, dist_sq = geometry(positions, target_pos, offset)
        radial_vals = radial(dist_sq, radial_count)[0]
        centred = (index == 13).astype(jnp.float32)
        radial_vals = radial_vals * (1.0 - centred * diagonal)
        weights = radial_vals.reshape(cell_shape + (slot_count, slot_count * radial_count)).astype(
            jnp.bfloat16
        )
        return message + jnp.einsum(
            "abcip,abcpd->abcid", weights, target_feat, preferred_element_type=jnp.float32
        )

    message = lax.fori_loop(
        0, 27, message_step, jnp.zeros(cell_shape + (slot_count, feature_width), jnp.float32)
    )
    message = MSG_SCALE * message
    sigmoid_msg = jax.nn.sigmoid(message)
    activated = (message * sigmoid_msg).astype(jnp.bfloat16)
    hidden = embedded.astype(jnp.float32) + jnp.einsum(
        "abcsd,de->abcse", activated, w_up, preferred_element_type=jnp.float32
    )
    energies = occupied * jnp.sum(hidden * w_energy, axis=-1)
    readout = jnp.sum(w_up.astype(jnp.float32) * w_energy[None, :], axis=1)
    adjoint = (
        occupied[..., None] * sigmoid_msg * (1.0 + message * (1.0 - sigmoid_msg)) * readout
    ).astype(jnp.bfloat16)
    adj_pad = with_halo(adjoint, (("gx", 0), ("gy", 1), ("gz", 2)), 1)

    def force_step(index, forces):
        offset = offset_of(index)
        target_pos = window(pos_pad, offset, cell_shape)
        target_feat = window(feat_pad, offset, cell_shape).reshape(grouped_shape)
        target_adj = window(adj_pad, offset, cell_shape)
        displace, dist_sq = geometry(positions, target_pos, offset)
        radial_slope = radial(dist_sq, radial_count)[1]
        outward = jnp.einsum(
            "abcid,abcpd->abcip", adjoint, target_feat, preferred_element_type=jnp.float32
        ).reshape(cell_shape + (slot_count, slot_count, radial_count))
        inward = jnp.einsum(
            "abcjd,abcpd->abcjp", target_adj, anchor_feat, preferred_element_type=jnp.float32
        ).reshape(cell_shape + (slot_count, slot_count, radial_count))
        inward = jnp.swapaxes(inward, -3, -2)
        pair_weight = MSG_SCALE * jnp.sum(radial_slope * (outward + inward), axis=-1)
        return forces + 2.0 * jnp.sum(displace * pair_weight[..., None, :, :], axis=-1)

    forces = lax.fori_loop(0, 27, force_step, jnp.zeros(cell_shape + (3, slot_count), jnp.float32))
    forces = (forces * occupied[..., None, :]).reshape(positions.shape)
    return (energies, forces)


def solution(mesh):
    in_specs = (
        P("gx", "gy", "gz", None),
        P("gx", "gy", "gz", None),
        P("gx", "gy", "gz"),
        P(),
        P(),
        P(),
        P(),
    )
    out_specs = (P("gx", "gy", "gz", None), P("gx", "gy", "gz", None))
    return jax.shard_map(
        on_device, mesh=mesh, in_specs=in_specs, out_specs=out_specs, check_vma=False
    )
```

profile of v0, /device:TPU:1, one launch (start us, length us, event | category | flops | bytes accessed | tf_op | source)
XLA Modules:
  0.0 341.0 jit_solution(11047998565685564060)
XLA Ops:
  3.3 5.9 %collective-permute-start.7 = (bf16[1,2,1,64,512]{4,3,1,2,0:T(8,128)(2,1)S(1)}, bf16[1,2,1,64,512]{4,3,1,2,0:T(8,128)(2,1)S(1)}, u32[]{:S(2)}, u32[]{:S(2)}) collective-permute-start(bf16[1,2,1,64,512]{4,3,1,2,0:T(8,128)(2,1)S(1)} %get-tuple-element.697), channel_id=1, source_target_pairs={{96,0},{192,96},{288,192},{384,288},{480,384},{576,480},{672,576},... | collective-permute-start | bytes 393224 | tf_op jit(solution)/shard_map/ppermute | solution.py:18
  9.3 1.9 collective-permute-start.6
  11.9 4.3 %collective-permute-done.6 = bf16[1,2,1,64,512]{4,3,1,0,2:T(8,128)(2,1)S(1)} collective-permute-done((bf16[1,2,1,64,512]{4,3,1,0,2:T(8,128)(2,1)S(1)}, bf16[1,2,1,64,512]{4,3,1,0,2:T(8,128)(2,1)S(1)}, u32[]{:S(2)}, u32[]{:S(2)}) %collective-permute-start.6) | collective-permute-done | bytes 131104 | tf_op jit(solution)/shard_map/ppermute | solution.py:15
  16.3 3.1 collective-permute-start.8
  19.4 8.6 %collective-permute-start.9 = (bf16[4,1,1,64,512]{4,3,1,0,2:T(8,128)(2,1)S(1)}, bf16[4,1,1,64,512]{4,3,1,0,2:T(8,128)(2,1)S(1)}, u32[]{:S(2)}, u32[]{:S(2)}) collective-permute-start(bf16[4,1,1,64,512]{4,3,1,0,2:T(8,128)(2,1)S(1)} %get-tuple-element.695), channel_id=1, source_target_pairs={{6,0},{12,6},{18,12},{24,18},{30,24},{36,30},{42,36},{48,42},{54,4... | collective-permute-start | bytes 786440 | tf_op jit(solution)/shard_map/ppermute | solution.py:18
  28.0 1.9 collective-permute-start
  30.0 4.6 %collective-permute-start.1 = (f32[1,2,1,192]{3,1,0,2:T(2,128)S(1)}, f32[1,2,1,192]{3,1,0,2:T(2,128)S(1)}, u32[]{:S(2)}, u32[]{:S(2)}) collective-permute-start(f32[1,2,1,192]{3,1,0,2:T(2,128)S(1)} %get-tuple-element.704), channel_id=1, source_target_pairs={{96,0},{192,96},{288,192},{384,288},{480,384},{576,480},{672,576},... | collective-permute-start | bytes 4616 | tf_op jit(solution)/shard_map/ppermute | solution.py:18
  34.7 13.2 %collective-permute-start.10 = (bf16[4,4,1,64,512]{4,3,1,0,2:T(8,128)(2,1)S(1)}, bf16[4,4,1,64,512]{4,3,1,0,2:T(8,128)(2,1)S(1)}, u32[]{:S(2)}, u32[]{:S(2)}) collective-permute-start(bf16[4,4,1,64,512]{4,3,1,0,2:T(8,128)(2,1)S(1)} %pad_maximum_fusion.1), channel_id=1, source_target_pairs={{0,1},{1,2},{2,3},{3,4},{4,5},{5,0},{6,7},{7,8},{8,9},{9,10},{10,1... | collective-permute-start | bytes 3145736 | tf_op jit(solution)/shard_map/ppermute | solution.py:15
  47.9 1.9 collective-permute-start.11
  49.9 1.9 collective-permute-start.2
  51.9 7.3 %collective-permute-start.3 = (f32[4,1,1,192]{3,1,0,2:T(1,128)S(1)}, f32[4,1,1,192]{3,1,0,2:T(1,128)S(1)}, u32[]{:S(2)}, u32[]{:S(2)}) collective-permute-start(f32[4,1,1,192]{3,1,0,2:T(1,128)S(1)} %get-tuple-element.703), channel_id=1, source_target_pairs={{6,0},{12,6},{18,12},{24,18},{30,24},{36,30},{42,36},{48,42},{54,4... | collective-permute-start | bytes 9224 | tf_op jit(solution)/shard_map/ppermute | solution.py:18
  60.2 5.4 %collective-permute-done.3 = f32[4,1,1,192]{3,1,0,2:T(1,128)S(1)} collective-permute-done((f32[4,1,1,192]{3,1,0,2:T(1,128)S(1)}, f32[4,1,1,192]{3,1,0,2:T(1,128)S(1)}, u32[]{:S(2)}, u32[]{:S(2)}) %collective-permute-start.3) | collective-permute-done | bytes 3104 | tf_op jit(solution)/shard_map/ppermute | solution.py:18
  65.6 38.4 %collective-permute-start.4 = (f32[4,4,1,192]{3,1,0,2:T(4,128)S(1)}, f32[4,4,1,192]{3,1,0,2:T(4,128)S(1)}, u32[]{:S(2)}, u32[]{:S(2)}) collective-permute-start(f32[4,4,1,192]{3,1,0,2:T(4,128)S(1)} %pad_maximum_fusion.7), channel_id=1, source_target_pairs={{0,1},{1,2},{2,3},{3,4},{4,5},{5,0},{6,7},{7,8},{8,9},{9,10},{10,1... | collective-permute-start | bytes 36872 | tf_op jit(solution)/shard_map/ppermute | solution.py:15
  104.1 1.9 collective-permute-start.5
  106.1 7.0 %collective-permute-done.5 = f32[4,4,1,192]{3,1,0,2:T(4,128)} collective-permute-done((f32[4,4,1,192]{3,1,0,2:T(4,128)S(1)}, f32[4,4,1,192]{3,1,0,2:T(4,128)}, u32[]{:S(2)}, u32[]{:S(2)}) %collective-permute-start.5) | collective-permute-done | bytes 12320 | tf_op jit(solution)/shard_map/ppermute | solution.py:18
  113.9 2.9 pad_maximum_fusion
  116.8 72.8 %while.38 = (s32[]{:T(128)}, f32[2,2,1,64,128]{4,3,1,0,2:T(8,128)S(1)}, f32[4,4,3,192]{3,1,0,2:T(4,128)S(1)}, f32[2,2,1,192]{3,1,0,2:T(2,128)S(1)}, bf16[4,4,3,6...) while((s32[]{:T(128)}, ...), condition=%wide.region_2.3_spmd.clone, body=%wide.region_0.2_spmd.clone.sunk | while | flops 17395772 | bytes 3404385 | solution.py:99
  117.8 1.0 constant_dynamic-slice_fusion.8
  123.2 1.0 constant_dynamic-slice_fusion.8
  131.3 1.0 constant_dynamic-slice_fusion.8
  134.0 1.0 constant_dynamic-slice_fusion.8
  136.7 1.0 constant_dynamic-slice_fusion.8
  189.7 1.9 collective-permute-start.12
  191.7 4.6 %collective-permute-start.13 = (bf16[1,2,1,64,128]{4,3,1,0,2:T(8,128)(2,1)S(1)}, bf16[1,2,1,64,128]{4,3,1,0,2:T(8,128)(2,1)S(1)}, u32[]{:S(2)}, u32[]{:S(2)}) collective-permute-start(bf16[1,2,1,64,128]{4,3,1,0,2:T(8,128)(2,1)S(1)} %get-tuple-element.701), channel_id=1, source_target_pairs={{96,0},{192,96},{288,192},{384,288},{480,384},{576,480},{672,576},... | collective-permute-start | bytes 98312 | tf_op jit(solution)/shard_map/ppermute | solution.py:18
  196.3 1.0 collective-permute-done.13
  197.3 1.9 collective-permute-start.14
  199.2 7.3 %collective-permute-start.15 = (bf16[4,1,1,64,128]{4,3,1,0,2:T(8,128)(2,1)S(1)}, bf16[4,1,1,64,128]{4,3,1,0,2:T(8,128)(2,1)S(1)}, u32[]{:S(2)}, u32[]{:S(2)}) collective-permute-start(bf16[4,1,1,64,128]{4,3,1,0,2:T(8,128)(2,1)S(1)} %get-tuple-element.699), channel_id=1, source_target_pairs={{6,0},{12,6},{18,12},{24,18},{30,24},{36,30},{42,36},{48,42},{54,4... | collective-permute-start | bytes 196616 | tf_op jit(solution)/shard_map/ppermute | solution.py:18
  206.7 2.2 collective-permute-done.15
  208.9 5.8 %collective-permute-start.16 = (bf16[4,4,1,64,128]{4,3,1,0,2:T(8,128)(2,1)S(1)}, bf16[4,4,1,64,128]{4,3,1,0,2:T(8,128)(2,1)S(1)}, u32[]{:S(2)}, u32[]{:S(2)}) collective-permute-start(bf16[4,4,1,64,128]{4,3,1,0,2:T(8,128)(2,1)S(1)} %pad_maximum_fusion.4), channel_id=1, source_target_pairs={{0,1},{1,2},{2,3},{3,4},{4,5},{5,0},{6,7},{7,8},{8,9},{9,10},{10,1... | collective-permute-start | bytes 786440 | tf_op jit(solution)/shard_map/ppermute | solution.py:15
  214.8 1.9 collective-permute-start.17
  218.0 10.1 %collective-permute-done.17 = bf16[4,4,1,64,128]{4,3,1,0,2:T(8,128)(2,1)S(1)} collective-permute-done((bf16[4,4,1,64,128]{4,3,1,0,2:T(8,128)(2,1)S(1)}, bf16[4,4,1,64,128]{4,3,1,0,2:T(8,128)(2,1)S(1)}, u32[]{:S(2)}, u32[]{:S(2)}) %collective-permute-start.17) | collective-permute-done | bytes 262176 | tf_op jit(solution)/shard_map/ppermute | solution.py:18
  228.3 112.0 %while.39 = (s32[]{:T(128)}, f32[2,2,1,3,64]{4,3,1,0,2:T(4,128)S(1)}, f32[4,4,3,192]{3,1,0,2:T(4,128)S(1)}, f32[2,2,1,192]{3,1,0,2:T(2,128)S(1)}, bf16[4,4,3,64,...) while((s32[]{:T(128)}, ...), condition=%wide.region_9.10_spmd.clone, body=%wide.region_5.9_spmd.clone.sunk | while | flops 34571828 | bytes 5089943 | solution.py:132
  (1108 shorter events, 176.5 us)
Async XLA Ops:
  0.6 2.5 copy-start
  0.6 58.5 %copy-start.6 = (s32[2,2,1]{1,2,0:T(1,128)S(1)}, s32[2,2,1]{1,2,0:T(1,128)}, u32[]{:S(2)}) copy-start(s32[2,2,1]{1,2,0:T(1,128)} %param.13) | copy-start | bytes 52
  0.7 49.2 %copy-start.5 = (f32[2,2,1,192]{3,2,1,0:T(1,128)S(1)}, f32[2,2,1,192]{3,2,1,0:T(1,128)}, u32[]{:S(2)}) copy-start(f32[2,2,1,192]{3,2,1,0:T(1,128)} %param.11) | copy-start | bytes 9220
  0.7 105.3 %copy-start.3 = (bf16[128,128]{1,0:T(8,128)(2,1)S(1)}, bf16[128,128]{1,0:T(8,128)(2,1)}, u32[]{:S(2)}) copy-start(bf16[128,128]{1,0:T(8,128)(2,1)} %param.16) | copy-start | bytes 98308
  0.7 105.3 %copy-start.7 = (f32[128]{0:T(128)S(1)}, f32[128]{0:T(128)}, u32[]{:S(2)}) copy-start(f32[128]{0:T(128)} %param.17) | copy-start | bytes 1540
  2.5 0.6 copy-start.1
  3.3 8.5 %collective-permute-start.7 = (bf16[1,2,1,64,512]{4,3,1,2,0:T(8,128)(2,1)S(1)}, bf16[1,2,1,64,512]{4,3,1,2,0:T(8,128)(2,1)S(1)}, u32[]{:S(2)}, u32[]{:S(2)}) collective-permute-start(bf16[1,2,1,64,512]{4,3,1,2,0:T(8,128)(2,1)S(1)} %get-tuple-element.697), channel_id=1, source_target_pairs={{96,0},{192,96},{288,192},{384,288},{480,384},{576,480},{672,576},... | collective-permute-start | bytes 393224 | tf_op jit(solution)/shard_map/ppermute | solution.py:18
  9.3 6.9 %collective-permute-start.6 = (bf16[1,2,1,64,512]{4,3,1,0,2:T(8,128)(2,1)S(1)}, bf16[1,2,1,64,512]{4,3,1,0,2:T(8,128)(2,1)S(1)}, u32[]{:S(2)}, u32[]{:S(2)}) collective-permute-start(bf16[1,2,1,64,512]{4,3,1,0,2:T(8,128)(2,1)S(1)} %get-tuple-element.696), channel_id=1, source_target_pairs={{0,96},{96,192},{192,288},{288,384},{384,480},{480,576},{576,672},... | collective-permute-start | bytes 393224 | tf_op jit(solution)/shard_map/ppermute | solution.py:15
  16.3 18.3 %collective-permute-start.8 = (bf16[4,1,1,64,512]{4,3,1,0,2:T(8,128)(2,1)S(1)}, bf16[4,1,1,64,512]{4,3,1,0,2:T(8,128)(2,1)S(1)}, u32[]{:S(2)}, u32[]{:S(2)}) collective-permute-start(bf16[4,1,1,64,512]{4,3,1,0,2:T(8,128)(2,1)S(1)} %get-tuple-element.694), channel_id=1, source_target_pairs={{0,6},{6,12},{12,18},{18,24},{24,30},{30,36},{36,42},{42,48},{48,5... | collective-permute-start | bytes 786440 | tf_op jit(solution)/shard_map/ppermute | solution.py:15
  19.4 15.2 %collective-permute-start.9 = (bf16[4,1,1,64,512]{4,3,1,0,2:T(8,128)(2,1)S(1)}, bf16[4,1,1,64,512]{4,3,1,0,2:T(8,128)(2,1)S(1)}, u32[]{:S(2)}, u32[]{:S(2)}) collective-permute-start(bf16[4,1,1,64,512]{4,3,1,0,2:T(8,128)(2,1)S(1)} %get-tuple-element.695), channel_id=1, source_target_pairs={{6,0},{12,6},{18,12},{24,18},{30,24},{36,30},{42,36},{48,42},{54,4... | collective-permute-start | bytes 786440 | tf_op jit(solution)/shard_map/ppermute | solution.py:18
  28.0 6.5 %collective-permute-start = (f32[1,2,1,192]{3,1,0,2:T(2,128)S(1)}, f32[1,2,1,192]{3,1,0,2:T(2,128)S(1)}, u32[]{:S(2)}, u32[]{:S(2)}) collective-permute-start(f32[1,2,1,192]{3,1,0,2:T(2,128)S(1)} %get-tuple-element.705), channel_id=1, source_target_pairs={{0,96},{96,192},{192,288},{288,384},{384,480},{480,576},{576,672},... | collective-permute-start | bytes 4616 | tf_op jit(solution)/shard_map/ppermute | solution.py:15
  30.0 19.9 %collective-permute-start.1 = (f32[1,2,1,192]{3,1,0,2:T(2,128)S(1)}, f32[1,2,1,192]{3,1,0,2:T(2,128)S(1)}, u32[]{:S(2)}, u32[]{:S(2)}) collective-permute-start(f32[1,2,1,192]{3,1,0,2:T(2,128)S(1)} %get-tuple-element.704), channel_id=1, source_target_pairs={{96,0},{192,96},{288,192},{384,288},{480,384},{576,480},{672,576},... | collective-permute-start | bytes 4616 | tf_op jit(solution)/shard_map/ppermute | solution.py:18
  34.7 79.1 %collective-permute-start.10 = (bf16[4,4,1,64,512]{4,3,1,0,2:T(8,128)(2,1)S(1)}, bf16[4,4,1,64,512]{4,3,1,0,2:T(8,128)(2,1)S(1)}, u32[]{:S(2)}, u32[]{:S(2)}) collective-permute-start(bf16[4,4,1,64,512]{4,3,1,0,2:T(8,128)(2,1)S(1)} %pad_maximum_fusion.1), channel_id=1, source_target_pairs={{0,1},{1,2},{2,3},{3,4},{4,5},{5,0},{6,7},{7,8},{8,9},{9,10},{10,1... | collective-permute-start | bytes 3145736 | tf_op jit(solution)/shard_map/ppermute | solution.py:15
  47.9 66.0 %collective-permute-start.11 = (bf16[4,4,1,64,512]{4,3,1,0,2:T(8,128)(2,1)S(1)}, bf16[4,4,1,64,512]{4,3,1,0,2:T(8,128)(2,1)}, u32[]{:S(2)}, u32[]{:S(2)}) collective-permute-start(bf16[4,4,1,64,512]{4,3,1,0,2:T(8,128)(2,1)S(1)} %pad_maximum_fusion.1), channel_id=1, source_target_pairs={{1,0},{2,1},{3,2},{4,3},{5,4},{0,5},{7,6},{8,7},{9,8},{10,9},{11,1... | collective-permute-start | bytes 3145736 | tf_op jit(solution)/shard_map/ppermute | solution.py:18
  49.9 10.3 %collective-permute-start.2 = (f32[4,1,1,192]{3,1,0,2:T(1,128)S(1)}, f32[4,1,1,192]{3,1,0,2:T(1,128)S(1)}, u32[]{:S(2)}, u32[]{:S(2)}) collective-permute-start(f32[4,1,1,192]{3,1,0,2:T(1,128)S(1)} %get-tuple-element.702), channel_id=1, source_target_pairs={{0,6},{6,12},{12,18},{18,24},{24,30},{30,36},{36,42},{42,48},{48,5... | collective-permute-start | bytes 9224 | tf_op jit(solution)/shard_map/ppermute | solution.py:15
  51.9 13.7 %collective-permute-start.3 = (f32[4,1,1,192]{3,1,0,2:T(1,128)S(1)}, f32[4,1,1,192]{3,1,0,2:T(1,128)S(1)}, u32[]{:S(2)}, u32[]{:S(2)}) collective-permute-start(f32[4,1,1,192]{3,1,0,2:T(1,128)S(1)} %get-tuple-element.703), channel_id=1, source_target_pairs={{6,0},{12,6},{18,12},{24,18},{30,24},{36,30},{42,36},{48,42},{54,4... | collective-permute-start | bytes 9224 | tf_op jit(solution)/shard_map/ppermute | solution.py:18
  65.6 40.5 %collective-permute-start.4 = (f32[4,4,1,192]{3,1,0,2:T(4,128)S(1)}, f32[4,4,1,192]{3,1,0,2:T(4,128)S(1)}, u32[]{:S(2)}, u32[]{:S(2)}) collective-permute-start(f32[4,4,1,192]{3,1,0,2:T(4,128)S(1)} %pad_maximum_fusion.7), channel_id=1, source_target_pairs={{0,1},{1,2},{2,3},{3,4},{4,5},{5,0},{6,7},{7,8},{8,9},{9,10},{10,1... | collective-permute-start | bytes 36872 | tf_op jit(solution)/shard_map/ppermute | solution.py:15
  104.1 9.1 %collective-permute-start.5 = (f32[4,4,1,192]{3,1,0,2:T(4,128)S(1)}, f32[4,4,1,192]{3,1,0,2:T(4,128)}, u32[]{:S(2)}, u32[]{:S(2)}) collective-permute-start(f32[4,4,1,192]{3,1,0,2:T(4,128)S(1)} %pad_maximum_fusion.7), channel_id=1, source_target_pairs={{1,0},{2,1},{3,2},{4,3},{5,4},{0,5},{7,6},{8,7},{9,8},{10,9},{11,1... | collective-permute-start | bytes 36872 | tf_op jit(solution)/shard_map/ppermute | solution.py:18
  116.8 99.9 %copy-start.2 = (bf16[2,2,64,128]{3,2,1,0:T(8,128)(2,1)S(1)}, bf16[2,2,64,128]{3,2,1,0:T(8,128)(2,1)}, u32[]{:S(2)}) copy-start(bf16[2,2,64,128]{3,2,1,0:T(8,128)(2,1)} %copy-done.1) | copy-start | bytes 196612
  116.8 99.9 %copy-start.4 = (bf16[128,128]{1,0:T(8,128)(2,1)S(1)}, bf16[128,128]{1,0:T(8,128)(2,1)}, u32[]{:S(2)}) copy-start(bf16[128,128]{1,0:T(8,128)(2,1)} %param.16) | copy-start | bytes 98308
  116.8 99.9 %copy-start.8 = (f32[128]{0:T(128)S(1)}, f32[128]{0:T(128)}, u32[]{:S(2)}) copy-start(f32[128]{0:T(128)} %param.17) | copy-start | bytes 1540
  189.7 6.5 %collective-permute-start.12 = (bf16[1,2,1,64,128]{4,3,1,0,2:T(8,128)(2,1)S(1)}, bf16[1,2,1,64,128]{4,3,1,0,2:T(8,128)(2,1)S(1)}, u32[]{:S(2)}, u32[]{:S(2)}) collective-permute-start(bf16[1,2,1,64,128]{4,3,1,0,2:T(8,128)(2,1)S(1)} %get-tuple-element.700), channel_id=1, source_target_pairs={{0,96},{96,192},{192,288},{288,384},{384,480},{480,576},{576,672},... | collective-permute-start | bytes 98312 | tf_op jit(solution)/shard_map/ppermute | solution.py:15
  191.7 5.6 %collective-permute-start.13 = (bf16[1,2,1,64,128]{4,3,1,0,2:T(8,128)(2,1)S(1)}, bf16[1,2,1,64,128]{4,3,1,0,2:T(8,128)(2,1)S(1)}, u32[]{:S(2)}, u32[]{:S(2)}) collective-permute-start(bf16[1,2,1,64,128]{4,3,1,0,2:T(8,128)(2,1)S(1)} %get-tuple-element.701), channel_id=1, source_target_pairs={{96,0},{192,96},{288,192},{384,288},{480,384},{576,480},{672,576},... | collective-permute-start | bytes 98312 | tf_op jit(solution)/shard_map/ppermute | solution.py:18
  197.3 9.4 %collective-permute-start.14 = (bf16[4,1,1,64,128]{4,3,1,0,2:T(8,128)(2,1)S(1)}, bf16[4,1,1,64,128]{4,3,1,0,2:T(8,128)(2,1)S(1)}, u32[]{:S(2)}, u32[]{:S(2)}) collective-permute-start(bf16[4,1,1,64,128]{4,3,1,0,2:T(8,128)(2,1)S(1)} %get-tuple-element.698), channel_id=1, source_target_pairs={{0,6},{6,12},{12,18},{18,24},{24,30},{30,36},{36,42},{42,48},{48,5... | collective-permute-start | bytes 196616 | tf_op jit(solution)/shard_map/ppermute | solution.py:15
  199.2 9.7 %collective-permute-start.15 = (bf16[4,1,1,64,128]{4,3,1,0,2:T(8,128)(2,1)S(1)}, bf16[4,1,1,64,128]{4,3,1,0,2:T(8,128)(2,1)S(1)}, u32[]{:S(2)}, u32[]{:S(2)}) collective-permute-start(bf16[4,1,1,64,128]{4,3,1,0,2:T(8,128)(2,1)S(1)} %get-tuple-element.699), channel_id=1, source_target_pairs={{6,0},{12,6},{18,12},{24,18},{30,24},{36,30},{42,36},{48,42},{54,4... | collective-permute-start | bytes 196616 | tf_op jit(solution)/shard_map/ppermute | solution.py:18
  208.9 9.1 %collective-permute-start.16 = (bf16[4,4,1,64,128]{4,3,1,0,2:T(8,128)(2,1)S(1)}, bf16[4,4,1,64,128]{4,3,1,0,2:T(8,128)(2,1)S(1)}, u32[]{:S(2)}, u32[]{:S(2)}) collective-permute-start(bf16[4,4,1,64,128]{4,3,1,0,2:T(8,128)(2,1)S(1)} %pad_maximum_fusion.4), channel_id=1, source_target_pairs={{0,1},{1,2},{2,3},{3,4},{4,5},{5,0},{6,7},{7,8},{8,9},{9,10},{10,1... | collective-permute-start | bytes 786440 | tf_op jit(solution)/shard_map/ppermute | solution.py:15
  214.8 13.4 %collective-permute-start.17 = (bf16[4,4,1,64,128]{4,3,1,0,2:T(8,128)(2,1)S(1)}, bf16[4,4,1,64,128]{4,3,1,0,2:T(8,128)(2,1)S(1)}, u32[]{:S(2)}, u32[]{:S(2)}) collective-permute-start(bf16[4,4,1,64,128]{4,3,1,0,2:T(8,128)(2,1)S(1)} %pad_maximum_fusion.4), channel_id=1, source_target_pairs={{1,0},{2,1},{3,2},{4,3},{5,4},{0,5},{7,6},{8,7},{9,8},{10,9},{11,1... | collective-permute-start | bytes 786440 | tf_op jit(solution)/shard_map/ppermute | solution.py:18
where the time goes:
time: 344 us; the launch traced here: 341 us
  starting transfers between devices  114 us (33%)
  local copies, waits for them, and re-layouts  109 us (32%)
  other arithmetic  50.7 us (15%)
  waiting for transfers between devices  31.4 us (9%)
  matrix products  22.8 us (7%)
  loops' own time  11.5 us (3%)
    ppermute x9, starting transfers between devices, with_halo(): lax.ppermute(lax.slice_in_dim(block, block.shape[dim] - width, None, axis...  70.2 us
    dynamic_slice x108, local copies, waits for them, and re-layouts, window(): lax.dynamic_slice(padded, starts, tuple(cell_shape) + padded.shape[3:])  53.7 us
    ppermute x9, starting transfers between devices, with_halo(): lax.ppermute(lax.slice_in_dim(block, 0, width, axis=dim), axis, backward)  44 us
    ppermute x9, waiting for transfers between devices, with_halo(): lax.ppermute(lax.slice_in_dim(block, 0, width, axis=dim), axis, backward)  25.7 us
    reduce_sum x27, other arithmetic, force_step(): jnp.sum(radial_slope * (outward + inward), axis=-1)  19.6 us
    dot_general x27, matrix products, message_step(): jnp.einsum('abcip,abcpd->abcid', weights, target_feat, preferred_element_...  9.98 us
    reduce_sum x54, other arithmetic, geometry(): return (displace, jnp.sum(displace * displace, axis=-3))  9.63 us
    reduce_sum x27, other arithmetic, force_step(): jnp.sum(displace * pair_weight[..., None, :, :], axis=-1)  9.19 us
  transfers between devices with their start and end apart: 18, of which 8 were waited for; matrix products, arithmetic and copies ran while one was open for 1% of the time, Pallas kernels for 0%

commit v1 on v0

v1 whole, which is shorter than its diff:
```python
import functools

import jax
import jax.numpy as jnp
from jax import lax
from jax.experimental import pallas as pl
from jax.experimental.pallas import tpu as pltpu
from jax.sharding import PartitionSpec as P

MESH = pl.DeviceIdType.MESH
F32 = jnp.float32
BF16 = jnp.bfloat16

SLOTS = 64
CH = 128
RAD = 4
SPEC = 128
MSG_SCALE = 0.1

CENTRE, NEAR, FAR = 0, 1, 2
NT = (((1,), (1,)), ((), ()))
NN = (((1,), (0,)), ((), ()))

DIRS = [
    (role, dx, dy)
    for role in (FAR, CENTRE, NEAR)
    for dx, dy in ((1, 1), (1, -1), (-1, 1), (-1, -1), (0, 1), (0, -1), (1, 0), (-1, 0), (0, 0))
    if (role, dx, dy) != (CENTRE, 0, 0)
]


def dot(a, b, dims=NN, precision=None):
    return lax.dot_general(a, b, dims, precision=precision, preferred_element_type=F32)


def pieces(values, count):
    out = []
    for _ in range(count):
        out.append(values.astype(BF16))
        values = values - out[-1].astype(F32)
    return out


def own_part(step):
    return {1: (1, 2), -1: (0, 1), 0: (0, 2)}[step]


def halo_part(step):
    return {1: (3, 4), -1: (0, 1), 0: (1, 3)}[step]


def near_tiles(c):
    ix, iy = c // 2, c % 2
    return [(ix + a) * 4 + iy + b for a in range(3) for b in range(3)]


def far_tiles(c):
    iy = c % 2
    return [16 + a * 4 + iy + b for a in range(2) for b in range(3)]


def kernel(
    sizes,
    cnt_ref,
    pos_ref,
    spec_ref,
    embed_ref,
    filt_ref,
    wup_ref,
    we_ref,
    en_ref,
    fo_ref,
    pad,
    rec,
    back,
    xz,
    ys,
    hot,
    anchor,
    table,
    rows,
    emb,
    wbuf,
    sbuf,
    abuf,
    act,
    racc,
    dacc,
    send1,
    recv1,
    send2,
    recv2,
):
    nx, ny, nz = sizes
    gx, gy, gz = (lax.axis_index(name) for name in ("gx", "gy", "gz"))
    odd = lax.rem(gz, 2)
    roles = (gz, gz + 1 - 2 * odd, lax.rem(gz + nz - 1 + 2 * odd, nz))

    def device(role, dx, dy):
        return (lax.rem(gx + nx + dx, nx), lax.rem(gy + ny + dy, ny), roles[role])

    barrier = pltpu.get_barrier_semaphore()
    for d in DIRS:
        pl.semaphore_signal(barrier, inc=1, device_id=device(*d), device_id_type=MESH)

    slot_lane = lax.broadcasted_iota(jnp.int32, (1, SLOTS), 1)
    for c in range(4):
        marked = jnp.where(slot_lane < cnt_ref[c], spec_ref[c : c + 1, :], -1).astype(F32)
        pad[CENTRE, 1 + c // 2, 1 + c % 2, 0:1, :] = pos_ref[c : c + 1, 0:128]
        pad[CENTRE, 1 + c // 2, 1 + c % 2, 1:2, :] = jnp.concatenate(
            [pos_ref[c : c + 1, 128:192], marked], axis=1
        )
    eye = lax.broadcasted_iota(jnp.int32, (SLOTS, SLOTS), 0) == lax.broadcasted_iota(
        jnp.int32, (SLOTS, SLOTS), 1
    )
    for c in range(4):
        for q in range(3):
            row = jnp.broadcast_to(pos_ref[c : c + 1, q * SLOTS : (q + 1) * SLOTS], (SLOTS, SLOTS))
            column = jnp.sum(jnp.where(eye, row, 0.0), axis=1, keepdims=True)
            shift = (1.0 + c // 2, 1.0 + c % 2, 0.0)[q]
            anchor[c, q] = jnp.broadcast_to(column + shift, (SLOTS, 128))
    emb[...] = jnp.zeros_like(emb)
    emb[0 : embed_ref.shape[0], :] = embed_ref[...].astype(F32)
    embedding = emb[...].astype(BF16)
    for k in range(RAD):
        table[k * SPEC : (k + 1) * SPEC, :] = dot(
            embedding, filt_ref[:, k * CH : (k + 1) * CH]
        ).astype(BF16)
    energy_rows = jnp.concatenate([p.astype(F32) for p in pieces(we_ref[...], 3)], axis=0).astype(BF16)
    rows[0:1, :] = jnp.sum(dot(energy_rows, wup_ref[...], NT), axis=0, keepdims=True)
    rows[1:2, :] = jnp.sum(dot(energy_rows, embedding, NT), axis=0, keepdims=True)

    pl.semaphore_wait(barrier, len(DIRS))

    def spread(n):
        role, dx, dy = DIRS[n]
        (xs, xe), (ys_, ye) = own_part(dx), own_part(dy)
        (tx, te), (ty, tf) = halo_part(-dx), halo_part(-dy)
        return pltpu.make_async_remote_copy(
            src_ref=pad.at[CENTRE, 1 + xs : 1 + xe, 1 + ys_ : 1 + ye],
            dst_ref=pad.at[role, tx:te, ty:tf],
            send_sem=send1.at[n],
            recv_sem=recv1.at[n],
            device_id=device(role, dx, dy),
            device_id_type=MESH,
        )

    out_copies = [spread(n) for n in range(len(DIRS))]
    for copy in out_copies:
        copy.start()

    lane2 = lax.broadcasted_iota(jnp.int32, (2, 128), 1)
    low2 = lane2 < SLOTS
    first2 = lax.broadcasted_iota(jnp.int32, (2, 128), 0) == 0
    species_row = lax.broadcasted_iota(jnp.int32, (SPEC, 128), 0).astype(F32)
    toward = (1 - 2 * odd).astype(F32)
    zoff = (jnp.zeros((), F32), toward, -toward)

    def pair_tile(t, cell_a, cell_b):
        (ra, xa, ya), (rb, xb, yb) = cell_a, cell_b
        a, b = pad[ra, xa, ya], pad[rb, xb, yb]
        a_swapped, b_swapped = pltpu.roll(a, SLOTS, 1), pltpu.roll(b, SLOTS, 1)
        offset = jnp.where(
            first2, jnp.where(low2, float(xa), float(xb)), jnp.where(low2, zoff[ra], zoff[rb])
        )
        xz[t] = jnp.where(low2, a, b_swapped) + offset
        mixed = jnp.where(low2, a_swapped, b)
        ys[t] = mixed + jnp.where(first2, jnp.where(low2, float(ya), float(yb)), 0.0)
        hot[t] = jnp.where(species_row == mixed[1:2, :], 1.0, 0.0).astype(BF16)

    def geometry(c, t, lo, size):
        dx = xz[t, 0:1, :] - anchor[c, 0, lo : lo + size, :]
        dy = ys[t, 0:1, :] - anchor[c, 1, lo : lo + size, :]
        dz = xz[t, 1:2, :] - anchor[c, 2, lo : lo + size, :]
        dist_sq = dx * dx + dy * dy + dz * dz
        falloff = jnp.maximum(1.0 - dist_sq, 0.0)
        return dx, dy, dz, falloff, jnp.exp(-0.5 * dist_sq)

    def weight_sums(c, tiles):
        for n, t in enumerate(tiles):
            for lo in range(0, SLOTS, 16):
                _, _, _, falloff, e0 = geometry(c, t, lo, 16)
                square = falloff * falloff
                if t == (1 + c // 2) * 4 + 1 + c % 2:
                    i = lax.broadcasted_iota(jnp.int32, (16, 128), 0) + lo
                    j = lax.broadcasted_iota(jnp.int32, (16, 128), 1)
                    square = jnp.where(i == j, 0.0, square)
                w = e0 * square
                u = e0 * e0
                u3 = u * u * u
                ladder = (u, u3, u3 * u3 * u3)
                for k in range(RAD):
                    wbuf[c, k * SLOTS + lo : k * SLOTS + lo + 16, n * 128 : (n + 1) * 128] = w.astype(BF16)
                    if k < RAD - 1:
                        w = w * ladder[k]
        onehot = jnp.concatenate([hot[t] for t in tiles], axis=1)
        return dot(wbuf[c, :, 0 : len(tiles) * 128], onehot, NT)

    def pair_forces(c, tiles, first):
        own = [[None] * (SLOTS // 8) for _ in range(3)]
        for t in tiles:
            onehot = hot[t]
            gathered = dot(abuf[c], jnp.concatenate([onehot, onehot], axis=0))
            other = [None] * 3
            for r in range(SLOTS // 8):
                dx, dy, dz, falloff, e0 = geometry(c, t, 8 * r, 8)
                u = e0 * e0
                u3 = u * u * u
                e1 = e0 * u
                e2 = e1 * u3
                e3 = e2 * (u3 * u3 * u3)
                q0, q1, q2, q3 = (
                    e * gathered[k * SLOTS + 8 * r : k * SLOTS + 8 * r + 8, :]
                    for k, e in enumerate((e0, e1, e2, e3))
                )
                plain = (q0 + q1) + (q2 + q3)
                graded = q0 + 3.0 * (q1 + 3.0 * (q2 + 3.0 * q3))
                pair = falloff * (falloff * graded + 4.0 * plain)
                for q, delta in enumerate((dx, dy, dz)):
                    term = pair * delta
                    own[q][r] = term if own[q][r] is None else own[q][r] + term
                    other[q] = term if other[q] is None else other[q] + term
            for q in range(3):
                racc[t, q] = racc[t, q] + other[q]
        for q in range(3):
            for r in range(SLOTS // 8):
                place = slice(q * SLOTS + 8 * r, q * SLOTS + 8 * r + 8)
                dacc[c, place, :] = own[q][r] if first else dacc[c, place, :] + own[q][r]

    def give_back(t, cell_a, cell_b):
        low = lax.broadcasted_iota(jnp.int32, (1, 128), 1) < SLOTS
        fx, fy, fz = (-jnp.sum(racc[t, q], axis=0, keepdims=True) for q in range(3))
        swap = lambda v: pltpu.roll(v, SLOTS, 1)
        ra, xa, ya = cell_a
        rb, xb, yb = cell_b
        back[ra, xa, ya, 0:1, :] = jnp.where(low, fx, swap(fy))
        back[ra, xa, ya, 1:2, :] = jnp.where(low, fz, 0.0)
        back[rb, xb, yb, 0:1, :] = jnp.where(low, swap(fx), fy)
        back[rb, xb, yb, 1:2, :] = jnp.where(low, swap(fz), 0.0)

    def collect(n):
        role, dx, dy = DIRS[n]
        (xs, xe), (ys_, ye) = halo_part(dx), halo_part(dy)
        return pltpu.make_async_remote_copy(
            src_ref=back.at[role, xs:xe, ys_:ye],
            dst_ref=rec.at[n, 0 : xe - xs, 0 : ye - ys_],
            send_sem=send2.at[n],
            recv_sem=recv2.at[n],
            device_id=device(role, dx, dy),
            device_id_type=MESH,
        )

    near_pairs = [(x * 4 + y, (CENTRE, x, y), (NEAR, x, y)) for x in range(4) for y in range(4)]
    far_pairs = [
        (16 + h * 4 + y, (FAR, 2 * h, y), (FAR, 2 * h + 1, y)) for h in range(2) for y in range(4)
    ]
    racc[...] = jnp.zeros_like(racc)

    for n, d in enumerate(DIRS):
        if d[0] != FAR:
            out_copies[n].wait_recv()
    for pair in near_pairs:
        pair_tile(*pair)
    for c in range(4):
        sbuf[c] = weight_sums(c, near_tiles(c))

    for n, d in enumerate(DIRS):
        if d[0] == FAR:
            out_copies[n].wait_recv()
    for pair in far_pairs:
        pair_tile(*pair)
    readout = rows[0:1, :]
    slot_row = lax.broadcasted_iota(jnp.int32, (SLOTS, CH), 0)
    for c in range(4):
        sums = sbuf[c] + weight_sums(c, far_tiles(c))
        wide = jnp.concatenate([sums[k * SLOTS : (k + 1) * SLOTS, :] for k in range(RAD)], axis=1)
        high, rest = pieces(wide, 2)
        both = dot(jnp.concatenate([high, rest], axis=0), table[...])
        message = MSG_SCALE * (both[0:SLOTS, :] + both[SLOTS : 2 * SLOTS, :])
        sigmoid = 1.0 / (1.0 + jnp.exp(-message))
        act[c] = (message * sigmoid).astype(BF16)
        occupied = (slot_row < cnt_ref[c]).astype(F32)
        adjoint = (occupied * sigmoid * (1.0 + message * (1.0 - sigmoid)) * readout).astype(BF16)
        slopes = -MSG_SCALE * dot(adjoint, table[...], NT)
        slopes = jnp.concatenate([slopes[:, k * SPEC : (k + 1) * SPEC] for k in range(RAD)], axis=0)
        abuf[c] = jnp.concatenate(pieces(slopes, 2), axis=1)
        pair_forces(c, far_tiles(c), True)
    for pair in far_pairs:
        give_back(*pair)
    back_copies = [collect(n) for n in range(len(DIRS))]
    for n, d in enumerate(DIRS):
        if d[0] == FAR:
            back_copies[n].start()
    for c in range(4):
        pair_forces(c, near_tiles(c), False)
    for pair in near_pairs:
        give_back(*pair)
    for n, d in enumerate(DIRS):
        if d[0] != FAR:
            back_copies[n].start()

    occupied_rows = [(slot_lane < cnt_ref[c]).astype(F32) for c in range(4)]
    readout_rows = jnp.concatenate([p.astype(F32) for p in pieces(rows[0:1, :], 3)], axis=0).astype(BF16)
    species_rows = jnp.concatenate([p.astype(F32) for p in pieces(rows[1:2, :], 3)], axis=0).astype(BF16)
    for c in range(4):
        centre = hot[(1 + c // 2) * 4 + 1 + c % 2]
        parts = dot(readout_rows, act[c], NT) + dot(species_rows, centre)[:, 0:SLOTS]
        en_ref[c : c + 1, :] = occupied_rows[c] * jnp.sum(parts, axis=0, keepdims=True)
    ones = jnp.ones((8, 128), F32)
    own = [dot(ones, dacc[c], NT, lax.Precision.HIGHEST)[0:1, :] for c in range(4)]
    for copy in back_copies:
        copy.wait_recv()
    for c in range(4):
        x, y = c // 2, c % 2
        total = back[CENTRE, 1 + x, 1 + y]
        for n, (role, dx, dy) in enumerate(DIRS):
            (xs, xe), (ys_, ye) = own_part(-dx), own_part(-dy)
            if xs <= x < xe and ys_ <= y < ye:
                total = total + rec[n, x - xs, y - ys_]
        planar = own[c][:, 0:128] + total[0:1, :]
        upright = own[c][:, 128:192] + total[1:2, 0:SLOTS]
        mask = occupied_rows[c]
        fo_ref[c : c + 1, 0:128] = planar * jnp.concatenate([mask, mask], axis=1)
        fo_ref[c : c + 1, 128:192] = upright * mask
    for copy in out_copies:
        copy.wait_send()
    for copy in back_copies:
        copy.wait_send()


def solution(mesh):
    sizes = tuple(mesh.shape[name] for name in ("gx", "gy", "gz"))
    in_specs = (
        P("gx", "gy", "gz", None),
        P("gx", "gy", "gz", None),
        P("gx", "gy", "gz"),
        P(),
        P(),
        P(),
        P(),
    )
    out_specs = (P("gx", "gy", "gz", None), P("gx", "gy", "gz", None))
    vmem = pl.BlockSpec(memory_space=pltpu.VMEM)
    smem = pl.BlockSpec(memory_space=pltpu.SMEM)
    count = len(DIRS)

    def on_device(positions, species, counts, embed, filters, w_up, w_energy):
        energies, forces = pl.pallas_call(
            functools.partial(kernel, sizes),
            out_shape=(
                jax.ShapeDtypeStruct((4, SLOTS), F32),
                jax.ShapeDtypeStruct((4, 3 * SLOTS), F32),
            ),
            in_specs=[smem] + [vmem] * 6,
            out_specs=(vmem, vmem),
            scratch_shapes=[
                pltpu.VMEM((3, 4, 4, 2, 128), F32),
                pltpu.VMEM((count, 2, 2, 2, 128), F32),
                pltpu.VMEM((3, 4, 4, 2, 128), F32),
                pltpu.VMEM((24, 2, 128), F32),
                pltpu.VMEM((24, 2, 128), F32),
                pltpu.VMEM((24, SPEC, 128), BF16),
                pltpu.VMEM((4, 3, SLOTS, 128), F32),
                pltpu.VMEM((RAD * SPEC, CH), BF16),
                pltpu.VMEM((8, 128), F32),
                pltpu.VMEM((SPEC, CH), F32),
                pltpu.VMEM((4, RAD * SLOTS, 9 * 128), BF16),
                pltpu.VMEM((4, RAD * SLOTS, SPEC), F32),
                pltpu.VMEM((4, RAD * SLOTS, 2 * SPEC), BF16),
                pltpu.VMEM((4, SLOTS, CH), BF16),
                pltpu.VMEM((24, 3, 8, 128), F32),
                pltpu.VMEM((4, 3 * SLOTS, 128), F32),
                pltpu.SemaphoreType.DMA((count,)),
                pltpu.SemaphoreType.DMA((count,)),
                pltpu.SemaphoreType.DMA((count,)),
                pltpu.SemaphoreType.DMA((count,)),
            ],
            compiler_params=pltpu.CompilerParams(
                collective_id=0, has_side_effects=True, vmem_limit_bytes=48 * 1024 * 1024
            ),
        )(
            counts.reshape(4),
            positions.reshape(4, 3 * SLOTS),
            species.reshape(4, SLOTS),
            embed,
            filters,
            w_up,
            w_energy.reshape(1, CH),
        )
        return energies.reshape(species.shape), forces.reshape(positions.shape)

    return jax.shard_map(
        on_device, mesh=mesh, in_specs=in_specs, out_specs=out_specs, check_vma=False
    )
```

time: 344 us -> 49.2 us (0.14)
  starting transfers between devices: 114 us -> 0 us
  local copies, waits for them, and re-layouts: 109 us -> 4.11 us
  other arithmetic: 50.7 us -> 2.05 us
  Pallas kernels: 0 us -> 42 us
  waiting for transfers between devices: 31.4 us -> 0 us
  matrix products: 22.8 us -> 0 us
  loops' own time: 11.5 us -> 0 us
    ppermute x18 -> x0, starting transfers between devices: 114 us -> none  [the longest x9 70.2 us: with_halo(): lax.ppermute(lax.slice_in_dim(block, block.shape[dim] - width, None, axis...]
    dynamic_slice x108 -> x0, local copies, waits for them, and re-layouts: 53.7 us -> none  [window(): lax.dynamic_slice(padded, starts, tuple(cell_shape) + padded.shape[3:])]
    pallas_call x0 -> x1, Pallas kernels: none -> 42 us  [on_device(): pl.pallas_call(functools.partial(kernel, sizes), out_shape=(jax.ShapeDtyp...]
    reduce_sum x109 -> x0, other arithmetic: 38.5 us -> none  [the longest x27 19.6 us: force_step(): jnp.sum(radial_slope * (outward + inward), axis=-1)]
    ppermute x18 -> x0, waiting for transfers between devices: 31.4 us -> none  [the longest x9 25.7 us: with_halo(): lax.ppermute(lax.slice_in_dim(block, 0, width, axis=dim), axis, backward)]
    dot_general x84 -> x0, matrix products: 22.8 us -> none  [the longest x27 9.98 us: message_step(): jnp.einsum('abcip,abcpd->abcid', weights, target_feat, preferred_element_...]
    mul x189 -> x0, local copies, waits for them, and re-layouts: 13.6 us -> none  [the longest x81 5.36 us: radial(): decaying = jnp.exp(-decay_rates * dist_sq[..., None])]
    another operation x2 -> x0, loops' own time: 11.5 us -> none  [the longest x1 5.77 us: on_device(): lax.fori_loop(0, 27, force_step, jnp.zeros(cell_shape + (3, slot_count),...]
  transfers between devices with their start and end apart: 18 -> 0, of which waited for: 8 -> 0; matrix products, arithmetic and copies ran while one was open for 1% -> 0% of each run, Pallas kernels for 0% -> 0%
where the time goes in v1:
time: 49.2 us; the launch traced here: 48.9 us
  Pallas kernels  42 us (85%)
  local copies, waits for them, and re-layouts  4.11 us (8%)
  other arithmetic  2.05 us (4%)
  between operations  0.67 us (1%)
    pallas_call x1, Pallas kernels, on_device(): pl.pallas_call(functools.partial(kernel, sizes), out_shape=(jax.ShapeDtyp...  42 us
    unnamed x12, local copies, waits for them, and re-layouts  3.4 us
    unnamed x2, other arithmetic  2.05 us

profile of v1, /device:TPU:1, one launch (start us, length us, event | category | flops | bytes accessed | tf_op | source)
XLA Modules:
  0.0 48.9 jit_solution(13621523413884107448)
XLA Ops:
  0.6 0.0 copy-start.2
  0.6 0.5 %broadcast.4 = s32[]{:T(128)} broadcast(s32[]{:T(128)} %constant.7), dimensions={} | broadcast | bytes 8 | tf_op args[2]
  1.2 1.3 %reduce.4 = s32[2,2]{1,0:T(2,128)S(1)} reduce(s32[2,2,1]{1,2,0:T(1,128)} %param.9, s32[]{:T(128)} %broadcast.4), dimensions={2}, to_apply=%param.9.reduce_sub_computation.3 | reduce | bytes 36 | tf_op args[2]
  2.5 0.1 reshape.22.cnt_ref
  2.6 0.7 %reduce.1 = f32[2,2,192]{2,1,0:T(2,128)S(1)} reduce(f32[2,2,1,192]{3,2,1,0:T(1,128)} %param.7, f32[]{:T(128)} %constant.4), dimensions={2}, to_apply=%param.7.reduce_sub_computation | reduce | bytes 6148 | tf_op args[0]
  3.3 0.0 copy-start.3
  3.3 0.0 copy-start.4
  3.3 0.0 copy-done.2
  3.3 0.6 %copy-done.3 = s32[2,2,1,64]{3,2,1,0:T(1,128)S(1)} copy-done((s32[2,2,1,64]{3,2,1,0:T(1,128)S(1)}, s32[2,2,1,64]{3,2,1,0:T(1,128)}, u32[]{:S(2)}) %copy-start.3) | copy-done | bytes 1048
  4.0 0.0 copy-done.4
  4.0 0.0 copy-start
  4.0 0.9 %copy-done = bf16[128,512]{1,0:T(8,128)(2,1)S(1)} copy-done((bf16[128,512]{1,0:T(8,128)(2,1)S(1)}, bf16[128,512]{1,0:T(8,128)(2,1)}, u32[]{:S(2)}) %copy-start) | copy-done | bytes 131096
  4.9 0.0 copy-start.1
  4.9 0.8 %copy-done.1 = bf16[128,128]{1,0:T(8,128)(2,1)S(1)} copy-done((bf16[128,128]{1,0:T(8,128)(2,1)S(1)}, bf16[128,128]{1,0:T(8,128)(2,1)}, u32[]{:S(2)}) %copy-start.1) | copy-done | bytes 32792
  5.6 42.0 %shard_map.86 = (f32[4,64]{1,0:T(4,128)S(1)}, f32[4,192]{1,0:T(4,128)S(1)}) custom-call(s32[4]{0:T(128)S(1)} %reshape.22.cnt_ref, f32[4,192]{1,0:T(4,128)S(1)} %reshape.23.pos_ref, s32[4,64]{1,0:T(4,128)S(1)} %bitcast.6, bf16[89,128]{1,0:T(8,128)(2,1)S(1)} %copy-done.2, bf16[128,512]{1,0:T(8,128)(2,1)S(1)} %copy-done, bf16[128,128]{1,0:T(8,128)(2,1)S(1)} %copy-done.1, ...), custom_call_target="tpu_custom_call" | custom-call | tf_op jit(solution)/shard_map/pallas_call | solution.py:348
  47.7 0.6 %reshape.28 = f32[2,2,1,192]{3,2,1,0:T(1,128)} reshape(f32[4,192]{1,0:T(4,128)S(1)} %get-tuple-element.5) | data formatting | bytes 6144 | tf_op jit(solution)/shard_map/reshape | solution.py:390
  48.3 0.6 %copy.13 = f32[2,2,1,64]{3,2,1,0:T(1,128)} copy(f32[2,2,1,64]{3,2,1,0:T(1,128)S(1)} %bitcast.7) | data formatting | bytes 2048
  (1 shorter events, 0.0 us)
Async XLA Ops:
  0.6 2.7 %copy-start.2 = (bf16[89,128]{1,0:T(8,128)(2,1)S(1)}, bf16[89,128]{1,0:T(8,128)(2,1)}, u32[]{:S(2)}) copy-start(bf16[89,128]{1,0:T(8,128)(2,1)} %embed_ref.1) | copy-start | bytes 68356
  3.3 0.7 %copy-start.3 = (s32[2,2,1,64]{3,2,1,0:T(1,128)S(1)}, s32[2,2,1,64]{3,2,1,0:T(1,128)}, u32[]{:S(2)}) copy-start(s32[2,2,1,64]{3,2,1,0:T(1,128)} %param.8) | copy-start | bytes 3076
  3.3 0.7 %copy-start.4 = (f32[128]{0:T(128)S(1)}, f32[128]{0:T(128)}, u32[]{:S(2)}) copy-start(f32[128]{0:T(128)} %param.13) | copy-start | bytes 1540
  4.0 0.9 %copy-start = (bf16[128,512]{1,0:T(8,128)(2,1)S(1)}, bf16[128,512]{1,0:T(8,128)(2,1)}, u32[]{:S(2)}) copy-start(bf16[128,512]{1,0:T(8,128)(2,1)} %filt_ref.1) | copy-start | bytes 393220
  4.9 0.8 %copy-start.1 = (bf16[128,128]{1,0:T(8,128)(2,1)S(1)}, bf16[128,128]{1,0:T(8,128)(2,1)}, u32[]{:S(2)}) copy-start(bf16[128,128]{1,0:T(8,128)(2,1)} %wup_ref.1) | copy-start | bytes 98308

commit v2 on v1

v2 whole, which is shorter than its diff:
```python
import functools

import jax
import jax.numpy as jnp
from jax import lax
from jax.experimental import pallas as pl
from jax.experimental.pallas import tpu as pltpu
from jax.sharding import PartitionSpec as P

MESH = pl.DeviceIdType.MESH
F32 = jnp.float32
BF16 = jnp.bfloat16

SLOTS = 64
CH = 128
RAD = 4
SPEC = 128
MSG_SCALE = 0.1
LOG2E = 1.4426950408889634
HALF = 0.5

CENTRE, NEAR, FAR = 0, 1, 2
NT = (((1,), (1,)), ((), ()))
NN = (((1,), (0,)), ((), ()))

DIRS = [
    (role, dx, dy)
    for role in (FAR, CENTRE, NEAR)
    for dx, dy in ((1, 1), (1, -1), (-1, 1), (-1, -1), (0, 1), (0, -1), (1, 0), (-1, 0), (0, 0))
    if (role, dx, dy) != (CENTRE, 0, 0)
]


def dot(a, b, dims=NN, precision=None):
    return lax.dot_general(a, b, dims, precision=precision, preferred_element_type=F32)


def pieces(values, count):
    out = []
    for _ in range(count):
        out.append(values.astype(BF16))
        values = values - out[-1].astype(F32)
    return out


def own_part(step):
    return {1: (1, 2), -1: (0, 1), 0: (0, 2)}[step]


def halo_part(step):
    return {1: (3, 4), -1: (0, 1), 0: (1, 3)}[step]


OWN_COLUMNS = [(x, y) for x in (1, 2) for y in (1, 2)]
PLANE_PAIRS = [((CENTRE, x, y), (NEAR, x, y)) for x in range(4) for y in range(4)]
FAR_PAIRS = [
    ((FAR,) + a, (FAR,) + b)
    for a, b in (
        ((0, 0), (1, 0)),
        ((2, 0), (3, 0)),
        ((3, 1), (3, 2)),
        ((3, 3), (2, 3)),
        ((1, 3), (0, 3)),
        ((0, 2), (0, 1)),
        ((1, 1), (1, 2)),
        ((2, 1), (2, 2)),
    )
]
PAIRS = PLANE_PAIRS + FAR_PAIRS


def tiles_of(c, wanted):
    x, y = 1 + c // 2, 1 + c % 2
    return [
        t
        for t, pair in enumerate(PAIRS)
        if wanted(pair) and any(abs(a - x) <= 1 and abs(b - y) <= 1 for _, a, b in pair)
    ]


def is_own(pair):
    return pair[0][0] != FAR and pair[0][1:] in OWN_COLUMNS


def is_side(pair):
    return pair[0][0] != FAR and pair[0][1:] not in OWN_COLUMNS


def is_far(pair):
    return pair[0][0] == FAR


def is_far_core(pair):
    return is_far(pair) and pair[0][1:] in OWN_COLUMNS


def is_far_ring(pair):
    return is_far(pair) and not is_far_core(pair)


def kernel(
    sizes,
    pos_hbm,
    spec_hbm,
    cnt_hbm,
    embed_hbm,
    filt_hbm,
    wup_hbm,
    we_hbm,
    en_ref,
    fo_ref,
    pos_ref,
    spec_ref,
    cnt_ref,
    embed_ref,
    filt_ref,
    wup_ref,
    we_ref,
    fetch,
    pad,
    rec,
    back,
    xz,
    ys,
    hot,
    anchor,
    table,
    rows,
    emb,
    sbuf,
    abuf,
    act,
    racc,
    dacc,
    send1,
    recv1,
    send2,
    recv2,
):
    nx, ny, nz = sizes
    gx, gy, gz = (lax.axis_index(name) for name in ("gx", "gy", "gz"))
    odd = lax.rem(gz, 2)
    roles = (gz, gz + 1 - 2 * odd, lax.rem(gz + nz - 1 + 2 * odd, nz))

    def device(role, dx, dy):
        return (lax.rem(gx + nx + dx, nx), lax.rem(gy + ny + dy, ny), roles[role])

    operands = [
        (pos_hbm, pos_ref),
        (spec_hbm, spec_ref),
        (cnt_hbm, cnt_ref),
        (embed_hbm, embed_ref),
        (filt_hbm, filt_ref),
        (wup_hbm, wup_ref),
        (we_hbm, we_ref),
    ]
    loads = [pltpu.make_async_copy(a, b, fetch.at[n]) for n, (a, b) in enumerate(operands)]
    for load in loads[0:3]:
        load.start()
    barrier = pltpu.get_barrier_semaphore()
    for d in DIRS:
        pl.semaphore_signal(barrier, inc=1, device_id=device(*d), device_id_type=MESH)
    for load in loads[3:]:
        load.start()
    for load in loads[0:3]:
        load.wait()

    slot_lane = lax.broadcasted_iota(jnp.int32, (1, SLOTS), 1)
    counts = [cnt_ref[c // 2, 0:1, c % 2 : c % 2 + 1] for c in range(4)]
    places = [pos_ref.at[c // 2, c % 2] for c in range(4)]
    for c in range(4):
        marked = jnp.where(slot_lane < counts[c], spec_ref[c // 2, c % 2], -1).astype(F32)
        pad[CENTRE, 1 + c // 2, 1 + c % 2, 0:1, :] = places[c][:, 0:128]
        pad[CENTRE, 1 + c // 2, 1 + c % 2, 1:2, :] = jnp.concatenate(
            [places[c][:, 128:192], marked], axis=1
        )
    eye = lax.broadcasted_iota(jnp.int32, (SLOTS, SLOTS), 0) == lax.broadcasted_iota(
        jnp.int32, (SLOTS, SLOTS), 1
    )
    for c in range(4):
        for q in range(3):
            row = jnp.broadcast_to(places[c][:, q * SLOTS : (q + 1) * SLOTS], (SLOTS, SLOTS))
            column = jnp.sum(jnp.where(eye, row, 0.0), axis=1, keepdims=True)
            shift = (1.0 + c // 2, 1.0 + c % 2, 0.0)[q]
            anchor[c, q] = jnp.broadcast_to(HALF * (column + shift), (SLOTS, 128))
    for load in loads[3:]:
        load.wait()
    emb[...] = jnp.zeros_like(emb)
    emb[0 : embed_ref.shape[0], :] = embed_ref[...].astype(F32)
    embedding = emb[...].astype(BF16)
    for k in range(RAD):
        table[k * SPEC : (k + 1) * SPEC, :] = dot(
            embedding, filt_ref[:, k * CH : (k + 1) * CH]
        ).astype(BF16)
    energy_rows = jnp.concatenate([p.astype(F32) for p in pieces(we_ref[...], 3)], axis=0).astype(BF16)
    rows[0:1, :] = jnp.sum(dot(energy_rows, wup_ref[...], NT), axis=0, keepdims=True)
    rows[1:2, :] = jnp.sum(dot(energy_rows, embedding, NT), axis=0, keepdims=True)

    pl.semaphore_wait(barrier, len(DIRS))

    def spread(n):
        role, dx, dy = DIRS[n]
        (xs, xe), (ys_, ye) = own_part(dx), own_part(dy)
        (tx, te), (ty, tf) = halo_part(-dx), halo_part(-dy)
        return pltpu.make_async_remote_copy(
            src_ref=pad.at[CENTRE, 1 + xs : 1 + xe, 1 + ys_ : 1 + ye],
            dst_ref=pad.at[role, tx:te, ty:tf],
            send_sem=send1.at[n],
            recv_sem=recv1.at[n],
            device_id=device(role, dx, dy),
            device_id_type=MESH,
        )

    out_copies = [spread(n) for n in range(len(DIRS))]
    for copy in out_copies:
        copy.start()

    lane2 = lax.broadcasted_iota(jnp.int32, (2, 128), 1)
    low2 = lane2 < SLOTS
    first2 = lax.broadcasted_iota(jnp.int32, (2, 128), 0) == 0
    species_row = lax.broadcasted_iota(jnp.int32, (SPEC, 128), 0).astype(F32)
    toward = (1 - 2 * odd).astype(F32)
    zoff = (jnp.zeros((), F32), toward, -toward)

    def pair_tile(t, cell_a, cell_b):
        (ra, xa, ya), (rb, xb, yb) = cell_a, cell_b
        a, b = pad[ra, xa, ya], pad[rb, xb, yb]
        a_swapped, b_swapped = pltpu.roll(a, SLOTS, 1), pltpu.roll(b, SLOTS, 1)
        offset = jnp.where(
            first2, jnp.where(low2, float(xa), float(xb)), jnp.where(low2, zoff[ra], zoff[rb])
        )
        xz[t] = HALF * (jnp.where(low2, a, b_swapped) + offset)
        mixed = jnp.where(low2, a_swapped, b)
        ys[t] = HALF * (mixed + jnp.where(first2, jnp.where(low2, float(ya), float(yb)), 0.0))
        hot[t] = jnp.where(species_row == mixed[1:2, :], 1.0, 0.0).astype(BF16)

    def geometry(c, t, lo, size):
        dx = xz[t, 0:1, :] - anchor[c, 0, lo : lo + size, :]
        dy = ys[t, 0:1, :] - anchor[c, 1, lo : lo + size, :]
        dz = xz[t, 1:2, :] - anchor[c, 2, lo : lo + size, :]
        dist_sq = dx * dx + dy * dy + dz * dz
        falloff = jnp.maximum(HALF * HALF - dist_sq, 0.0)
        decaying = [jnp.exp2((-0.5 * LOG2E * 3.0**k / HALF**2) * dist_sq) for k in range(RAD)]
        return dx, dy, dz, falloff, decaying

    def weight_sums(c, tiles):
        columns = []
        for t in tiles:
            blocks = [[] for _ in range(RAD)]
            for lo in range(0, SLOTS, 16):
                _, _, _, falloff, decaying = geometry(c, t, lo, 16)
                square = falloff * falloff
                if t == (1 + c // 2) * 4 + 1 + c % 2:
                    i = lax.broadcasted_iota(jnp.int32, (16, 128), 0) + lo
                    j = lax.broadcasted_iota(jnp.int32, (16, 128), 1)
                    square = jnp.where(i == j, 0.0, square)
                for k in range(RAD):
                    blocks[k].append((decaying[k] * square).astype(BF16))
            columns.append(jnp.concatenate(sum(blocks, []), axis=0))
        onehot = jnp.concatenate([hot[t] for t in tiles], axis=1)
        return dot(jnp.concatenate(columns, axis=1), onehot, NT)

    def pair_forces(c, tiles, first):
        own = [[None] * (SLOTS // 8) for _ in range(3)]
        for start in range(0, len(tiles), 2):
            group = tiles[start : start + 2]
            onehot = jnp.concatenate([hot[t] for t in group], axis=1)
            gathered = dot(abuf[c], jnp.concatenate([onehot, onehot], axis=0))
            for n, t in enumerate(group):
                other = [None] * 3
                for r in range(SLOTS // 8):
                    dx, dy, dz, falloff, decaying = geometry(c, t, 8 * r, 8)
                    q0, q1, q2, q3 = (
                        e * gathered[k * SLOTS + 8 * r : k * SLOTS + 8 * r + 8, n * 128 : (n + 1) * 128]
                        for k, e in enumerate(decaying)
                    )
                    plain = (q0 + q1) + (q2 + q3)
                    graded = q0 + 3.0 * (q1 + 3.0 * (q2 + 3.0 * q3))
                    pair = falloff * (falloff * graded + plain)
                    for q, delta in enumerate((dx, dy, dz)):
                        term = pair * delta
                        own[q][r] = term if own[q][r] is None else own[q][r] + term
                        other[q] = term if other[q] is None else other[q] + term
                for q in range(3):
                    racc[t, q] = racc[t, q] + other[q]
        for q in range(3):
            for r in range(SLOTS // 8):
                place = slice(q * SLOTS + 8 * r, q * SLOTS + 8 * r + 8)
                dacc[c, place, :] = own[q][r] if first else dacc[c, place, :] + own[q][r]

    def give_back(t, cell_a, cell_b):
        low = lax.broadcasted_iota(jnp.int32, (1, 128), 1) < SLOTS
        fx, fy, fz = (-jnp.sum(racc[t, q], axis=0, keepdims=True) for q in range(3))
        swap = lambda v: pltpu.roll(v, SLOTS, 1)
        ra, xa, ya = cell_a
        rb, xb, yb = cell_b
        back[ra, xa, ya, 0:1, :] = jnp.where(low, fx, swap(fy))
        back[ra, xa, ya, 1:2, :] = jnp.where(low, fz, 0.0)
        back[rb, xb, yb, 0:1, :] = jnp.where(low, swap(fx), fy)
        back[rb, xb, yb, 1:2, :] = jnp.where(low, swap(fz), 0.0)

    def collect(n):
        role, dx, dy = DIRS[n]
        (xs, xe), (ys_, ye) = halo_part(dx), halo_part(dy)
        return pltpu.make_async_remote_copy(
            src_ref=back.at[role, xs:xe, ys_:ye],
            dst_ref=rec.at[n, 0 : xe - xs, 0 : ye - ys_],
            send_sem=send2.at[n],
            recv_sem=recv2.at[n],
            device_id=device(role, dx, dy),
            device_id_type=MESH,
        )

    racc[...] = jnp.zeros_like(racc)
    own_tiles = [tiles_of(c, is_own) for c in range(4)]
    side_tiles = [tiles_of(c, is_side) for c in range(4)]
    far_tiles = [tiles_of(c, is_far) for c in range(4)]

    mate = (NEAR, 0, 0)
    out_copies[DIRS.index(mate)].wait_recv()
    for t, pair in enumerate(PAIRS):
        if is_own(pair):
            pair_tile(t, *pair)
    for c in range(4):
        sbuf[c] = weight_sums(c, own_tiles[c])

    for n, d in enumerate(DIRS):
        if d[0] != FAR and d != mate:
            out_copies[n].wait_recv()
    for t, pair in enumerate(PAIRS):
        if is_side(pair):
            pair_tile(t, *pair)
    for c in range(4):
        sbuf[c] = sbuf[c] + weight_sums(c, side_tiles[c])

    for n, d in enumerate(DIRS):
        if d[0] == FAR:
            out_copies[n].wait_recv()
    for t, pair in enumerate(PAIRS):
        if is_far(pair):
            pair_tile(t, *pair)
    readout = rows[0:1, :]
    slot_row = lax.broadcasted_iota(jnp.int32, (SLOTS, CH), 0)
    for c in range(4):
        sbuf[c] = sbuf[c] + weight_sums(c, far_tiles[c])
    for c in range(4):
        sums = sbuf[c]
        wide = jnp.concatenate([sums[k * SLOTS : (k + 1) * SLOTS, :] for k in range(RAD)], axis=1)
        high, rest = pieces(wide, 2)
        both = dot(jnp.concatenate([high, rest], axis=0), table[...])
        message = (MSG_SCALE / HALF**4) * (both[0:SLOTS, :] + both[SLOTS : 2 * SLOTS, :])
        sigmoid = 1.0 / (1.0 + jnp.exp(-message))
        act[c] = (message * sigmoid).astype(BF16)
        occupied = (slot_row < counts[c]).astype(F32)
        adjoint = (occupied * sigmoid * (1.0 + message * (1.0 - sigmoid)) * readout).astype(BF16)
        slopes = (-MSG_SCALE * 4 / HALF**3) * dot(adjoint, table[...], NT)
        slopes = jnp.concatenate([slopes[:, k * SPEC : (k + 1) * SPEC] for k in range(RAD)], axis=0)
        abuf[c] = jnp.concatenate(pieces(slopes, 2), axis=1)
    back_copies = [collect(n) for n in range(len(DIRS))]

    def react(wanted, sends, first=False):
        for c in range(4):
            pair_forces(c, tiles_of(c, wanted), first)
        for t, pair in enumerate(PAIRS):
            if wanted(pair):
                give_back(t, *pair)
        for n, d in enumerate(DIRS):
            if sends(d):
                back_copies[n].start()

    react(is_far_ring, lambda d: d[0] == FAR and d[1:] != (0, 0), True)
    react(is_side, lambda d: d[0] != FAR and d[1:] != (0, 0))
    react(is_far_core, lambda d: d == (FAR, 0, 0))
    react(is_own, lambda d: d == (NEAR, 0, 0))

    occupied_rows = [(slot_lane < counts[c]).astype(F32) for c in range(4)]
    readout_rows = jnp.concatenate([p.astype(F32) for p in pieces(rows[0:1, :], 3)], axis=0).astype(BF16)
    species_rows = jnp.concatenate([p.astype(F32) for p in pieces(rows[1:2, :], 3)], axis=0).astype(BF16)
    for c in range(4):
        centre = hot[(1 + c // 2) * 4 + 1 + c % 2]
        parts = dot(readout_rows, act[c], NT) + dot(species_rows, centre)[:, 0:SLOTS]
        en_ref[c // 2, c % 2] = occupied_rows[c] * jnp.sum(parts, axis=0, keepdims=True)
    ones = jnp.ones((8, 128), F32)
    own = [dot(ones, dacc[c], NT, lax.Precision.HIGHEST)[0:1, :] for c in range(4)]
    for copy in back_copies:
        copy.wait_recv()
    for c in range(4):
        x, y = c // 2, c % 2
        total = back[CENTRE, 1 + x, 1 + y]
        for n, (role, dx, dy) in enumerate(DIRS):
            (xs, xe), (ys_, ye) = own_part(-dx), own_part(-dy)
            if xs <= x < xe and ys_ <= y < ye:
                total = total + rec[n, x - xs, y - ys_]
        planar = own[c][:, 0:128] + total[0:1, :]
        upright = own[c][:, 128:192] + total[1:2, 0:SLOTS]
        mask = occupied_rows[c]
        fo_ref[c // 2, c % 2, :, 0:128] = planar * jnp.concatenate([mask, mask], axis=1)
        fo_ref[c // 2, c % 2, :, 128:192] = upright * mask
    for copy in out_copies:
        copy.wait_send()
    for copy in back_copies:
        copy.wait_send()


def solution(mesh):
    sizes = tuple(mesh.shape[name] for name in ("gx", "gy", "gz"))
    in_specs = (
        P("gx", "gy", "gz", None),
        P("gx", "gy", "gz", None),
        P("gx", "gy", "gz"),
        P(),
        P(),
        P(),
        P(),
    )
    out_specs = (P("gx", "gy", "gz", None), P("gx", "gy", "gz", None))
    vmem = pl.BlockSpec(memory_space=pltpu.VMEM)
    anywhere = pl.BlockSpec(memory_space=pl.ANY)
    count = len(DIRS)

    def on_device(positions, species, counts, embed, filters, w_up, w_energy):
        operands = (
            positions,
            species,
            counts.transpose(0, 2, 1),
            embed,
            filters,
            w_up,
            w_energy.reshape(1, CH),
        )
        operands = [pltpu.with_memory_space_constraint(a, pltpu.HBM) for a in operands]
        return pl.pallas_call(
            functools.partial(kernel, sizes),
            out_shape=(
                jax.ShapeDtypeStruct(species.shape, F32),
                jax.ShapeDtypeStruct(positions.shape, F32),
            ),
            in_specs=[anywhere] * len(operands),
            out_specs=(vmem, vmem),
            scratch_shapes=[pltpu.VMEM(a.shape, a.dtype) for a in operands]
            + [
                pltpu.SemaphoreType.DMA((len(operands),)),
                pltpu.VMEM((3, 4, 4, 2, 128), F32),
                pltpu.VMEM((count, 2, 2, 2, 128), F32),
                pltpu.VMEM((3, 4, 4, 2, 128), F32),
                pltpu.VMEM((24, 2, 128), F32),
                pltpu.VMEM((24, 2, 128), F32),
                pltpu.VMEM((24, SPEC, 128), BF16),
                pltpu.VMEM((4, 3, SLOTS, 128), F32),
                pltpu.VMEM((RAD * SPEC, CH), BF16),
                pltpu.VMEM((8, 128), F32),
                pltpu.VMEM((SPEC, CH), F32),
                pltpu.VMEM((4, RAD * SLOTS, SPEC), F32),
                pltpu.VMEM((4, RAD * SLOTS, 2 * SPEC), BF16),
                pltpu.VMEM((4, SLOTS, CH), BF16),
                pltpu.VMEM((24, 3, 8, 128), F32),
                pltpu.VMEM((4, 3 * SLOTS, 128), F32),
                pltpu.SemaphoreType.DMA((count,)),
                pltpu.SemaphoreType.DMA((count,)),
                pltpu.SemaphoreType.DMA((count,)),
                pltpu.SemaphoreType.DMA((count,)),
            ],
            compiler_params=pltpu.CompilerParams(
                collective_id=0, has_side_effects=True, vmem_limit_bytes=48 * 1024 * 1024
            ),
        )(*operands)

    return jax.shard_map(
        on_device, mesh=mesh, in_specs=in_specs, out_specs=out_specs, check_vma=False
    )
```

time: 49.2 us -> 41 us (0.83)
  Pallas kernels: 42 us -> 39 us
  local copies, waits for them, and re-layouts: 4.11 us -> 1.17 us
  other arithmetic: 2.05 us -> 0 us
    pallas_call x1, Pallas kernels: 42 us -> 39 us  [on_device(): pl.pallas_call(functools.partial(kernel, sizes), out_shape=(jax.ShapeDtyp...]
    unnamed x12 -> x2, local copies, waits for them, and re-layouts: 3.4 us -> 1.17 us
    unnamed x2 -> x0, other arithmetic: 2.05 us -> none
    reshape x3 -> x0, local copies, waits for them, and re-layouts: 0.71 us -> none  [the longest x1 0.61 us: on_device(): return (energies.reshape(species.shape), forces.reshape(positions.shape))]
where the time goes in v2:
time: 41 us; the launch traced here: 40.8 us
  Pallas kernels  39 us (95%)
  local copies, waits for them, and re-layouts  1.17 us (3%)
  between operations  0.64 us (2%)
    pallas_call x1, Pallas kernels, on_device(): pl.pallas_call(functools.partial(kernel, sizes), out_shape=(jax.ShapeDtyp...  39 us
    unnamed x2, local copies, waits for them, and re-layouts  1.17 us

profile of v2, /device:TPU:1, one launch (start us, length us, event | category | flops | bytes accessed | tf_op | source)
XLA Modules:
  0.0 40.8 jit_solution(9369112192768645871)
XLA Ops:
  0.6 39.0 %shard_map.86 = (f32[2,2,1,64]{3,2,1,0:T(1,128)S(1)}, f32[2,2,1,192]{3,2,1,0:T(1,128)S(1)}) custom-call(f32[2,2,1,192]{3,2,1,0:T(1,128)} %pos_hbm.1, s32[2,2,1,64]{3,2,1,0:T(1,128)} %spec_hbm.1, s32[2,1,2]{2,1,0:T(1,128)} %bitcast.4, bf16[89,128]{1,0:T(8,128)(2,1)} %embed_hbm.1, bf16[128,512]{1,0:T(8,128)(2,1)} %filt_hbm.1, bf16[128,128]{1,0:T(8,128)(2,1)} %wup_hbm.1, ...), custom_call_target="tpu_custom_call" | custom-call | tf_op jit(solution)/shard_map/pallas_call | solution.py:432
  39.7 0.6 %copy.12 = f32[2,2,1,64]{3,2,1,0:T(1,128)} copy(f32[2,2,1,64]{3,2,1,0:T(1,128)S(1)} %get-tuple-element.4) | data formatting | bytes 2048
  40.3 0.6 %copy.13 = f32[2,2,1,192]{3,2,1,0:T(1,128)} copy(f32[2,2,1,192]{3,2,1,0:T(1,128)S(1)} %get-tuple-element.5) | data formatting | bytes 6144

commit v3 on v2

--- a/solution.py
+++ b/solution.py
@@ -18,6 +18,8 @@
 MSG_SCALE = 0.1
 LOG2E = 1.4426950408889634
 HALF = 0.5
+
+FORCE_SCALE = -MSG_SCALE * 4 / HALF**3
 
 CENTRE, NEAR, FAR = 0, 1, 2
 NT = (((1,), (1,)), ((), ()))
@@ -96,6 +98,11 @@
 
 def is_far_ring(pair):
     return is_far(pair) and not is_far_core(pair)
+
+
+def corner_of(c):
+    cell = (FAR, 3 * (c // 2), 3 * (c % 2))
+    return next((t, pair.index(cell)) for t, pair in enumerate(PAIRS) if cell in pair)
 
 
 def kernel(
@@ -288,16 +295,18 @@
                 place = slice(q * SLOTS + 8 * r, q * SLOTS + 8 * r + 8)
                 dacc[c, place, :] = own[q][r] if first else dacc[c, place, :] + own[q][r]
 
-    def give_back(t, cell_a, cell_b):
+    def give_back(t, halves=(0, 1)):
         low = lax.broadcasted_iota(jnp.int32, (1, 128), 1) < SLOTS
-        fx, fy, fz = (-jnp.sum(racc[t, q], axis=0, keepdims=True) for q in range(3))
+        fx, fy, fz = (-FORCE_SCALE * jnp.sum(racc[t, q], axis=0, keepdims=True) for q in range(3))
         swap = lambda v: pltpu.roll(v, SLOTS, 1)
-        ra, xa, ya = cell_a
-        rb, xb, yb = cell_b
-        back[ra, xa, ya, 0:1, :] = jnp.where(low, fx, swap(fy))
-        back[ra, xa, ya, 1:2, :] = jnp.where(low, fz, 0.0)
-        back[rb, xb, yb, 0:1, :] = jnp.where(low, swap(fx), fy)
-        back[rb, xb, yb, 1:2, :] = jnp.where(low, swap(fz), 0.0)
+        for half in halves:
+            r, x, y = PAIRS[t][half]
+            if half:
+                back[r, x, y, 0:1, :] = jnp.where(low, swap(fx), fy)
+                back[r, x, y, 1:2, :] = jnp.where(low, swap(fz), 0.0)
+            else:
+                back[r, x, y, 0:1, :] = jnp.where(low, fx, swap(fy))
+                back[r, x, y, 1:2, :] = jnp.where(low, fz, 0.0)
 
     def collect(n):
         role, dx, dy = DIRS[n]
@@ -312,66 +321,78 @@
         )
 
     racc[...] = jnp.zeros_like(racc)
-    own_tiles = [tiles_of(c, is_own) for c in range(4)]
-    side_tiles = [tiles_of(c, is_side) for c in range(4)]
-    far_tiles = [tiles_of(c, is_far) for c in range(4)]
-
-    mate = (NEAR, 0, 0)
-    out_copies[DIRS.index(mate)].wait_recv()
-    for t, pair in enumerate(PAIRS):
-        if is_own(pair):
-            pair_tile(t, *pair)
-    for c in range(4):
-        sbuf[c] = weight_sums(c, own_tiles[c])
-
-    for n, d in enumerate(DIRS):
-        if d[0] != FAR and d != mate:
-            out_copies[n].wait_recv()
-    for t, pair in enumerate(PAIRS):
-        if is_side(pair):
-            pair_tile(t, *pair)
-    for c in range(4):
-        sbuf[c] = sbuf[c] + weight_sums(c, side_tiles[c])
-
-    for n, d in enumerate(DIRS):
-        if d[0] == FAR:
-            out_copies[n].wait_recv()
-    for t, pair in enumerate(PAIRS):
-        if is_far(pair):
-            pair_tile(t, *pair)
-    readout = rows[0:1, :]
+
+    def arrive(wanted):
+        for n, d in enumerate(DIRS):
+            if wanted(d):
+                out_copies[n].wait_recv()
+
+    def take_in(wanted, first=False):
+        for t, pair in enumerate(PAIRS):
+            if wanted(pair):
+                pair_tile(t, *pair)
+        for c in range(4):
+            part = weight_sums(c, tiles_of(c, wanted))
+            sbuf[c] = part if first else sbuf[c] + part
+
+    arrive(lambda d: d == (NEAR, 0, 0))
+    take_in(is_own, True)
+    arrive(lambda d: d[0] != FAR and d != (NEAR, 0, 0))
+    take_in(is_side)
+    arrive(lambda d: d == (FAR, 0, 0))
+    take_in(is_far_core)
+    arrive(lambda d: d[0] == FAR and d[1:] != (0, 0))
+    take_in(is_far_ring)
+
     slot_row = lax.broadcasted_iota(jnp.int32, (SLOTS, CH), 0)
-    for c in range(4):
-        sbuf[c] = sbuf[c] + weight_sums(c, far_tiles[c])
+    split = []
     for c in range(4):
         sums = sbuf[c]
         wide = jnp.concatenate([sums[k * SLOTS : (k + 1) * SLOTS, :] for k in range(RAD)], axis=1)
-        high, rest = pieces(wide, 2)
-        both = dot(jnp.concatenate([high, rest], axis=0), table[...])
-        message = (MSG_SCALE / HALF**4) * (both[0:SLOTS, :] + both[SLOTS : 2 * SLOTS, :])
-        sigmoid = 1.0 / (1.0 + jnp.exp(-message))
-        act[c] = (message * sigmoid).astype(BF16)
-        occupied = (slot_row < counts[c]).astype(F32)
-        adjoint = (occupied * sigmoid * (1.0 + message * (1.0 - sigmoid)) * readout).astype(BF16)
-        slopes = (-MSG_SCALE * 4 / HALF**3) * dot(adjoint, table[...], NT)
-        slopes = jnp.concatenate([slopes[:, k * SPEC : (k + 1) * SPEC] for k in range(RAD)], axis=0)
-        abuf[c] = jnp.concatenate(pieces(slopes, 2), axis=1)
+        split += pieces(wide, 2)
+    both = dot(jnp.concatenate(split, axis=0), table[...])
+    message = jnp.concatenate(
+        [both[c * 128 : c * 128 + 64, :] + both[c * 128 + 64 : c * 128 + 128, :] for c in range(4)], axis=0
+    )
+    message = (MSG_SCALE / HALF**4) * message
+    sigmoid = 1.0 / (1.0 + jnp.exp(-message))
+    act[...] = (message * sigmoid).astype(BF16).reshape(act.shape)
+    occupied = jnp.concatenate([(slot_row < counts[c]).astype(F32) for c in range(4)], axis=0)
+    adjoint = (occupied * sigmoid * (1.0 + message * (1.0 - sigmoid)) * rows[0:1, :]).astype(BF16)
+    slopes = dot(adjoint, table[...], NT)
+    for c in range(4):
+        mine = slopes[c * SLOTS : (c + 1) * SLOTS, :]
+        mine = jnp.concatenate([mine[:, k * SPEC : (k + 1) * SPEC] for k in range(RAD)], axis=0)
+        abuf[c] = jnp.concatenate(pieces(mine, 2), axis=1)
     back_copies = [collect(n) for n in range(len(DIRS))]
 
-    def react(wanted, sends, first=False):
+    def send_back(wanted):
+        for n, d in enumerate(DIRS):
+            if wanted(d):
+                back_copies[n].start()
+
+    corners = [corner_of(c) for c in range(4)]
+    for c in range(4):
+        pair_forces(c, [corners[c][0]], True)
+    for t, half in corners:
+        give_back(t, (half,))
+    send_back(lambda d: d[0] == FAR and 0 not in d[1:])
+
+    def react(wanted):
         for c in range(4):
-            pair_forces(c, tiles_of(c, wanted), first)
+            pair_forces(c, [t for t in tiles_of(c, wanted) if t != corners[c][0]], False)
         for t, pair in enumerate(PAIRS):
             if wanted(pair):
-                give_back(t, *pair)
-        for n, d in enumerate(DIRS):
-            if sends(d):
-                back_copies[n].start()
-
-    react(is_far_ring, lambda d: d[0] == FAR and d[1:] != (0, 0), True)
-    react(is_side, lambda d: d[0] != FAR and d[1:] != (0, 0))
-    react(is_far_core, lambda d: d == (FAR, 0, 0))
-    react(is_own, lambda d: d == (NEAR, 0, 0))
+                give_back(t, [h for h in (0, 1) if (t, h) not in corners])
+
+    react(is_far_ring)
+    send_back(lambda d: d[0] == FAR and d[1:].count(0) == 1)
+    react(is_side)
+    send_back(lambda d: d[0] != FAR and d[1:] != (0, 0))
+    react(is_far_core)
+    send_back(lambda d: d == (FAR, 0, 0))
+    react(is_own)
+    send_back(lambda d: d == (NEAR, 0, 0))
 
     occupied_rows = [(slot_lane < counts[c]).astype(F32) for c in range(4)]
     readout_rows = jnp.concatenate([p.astype(F32) for p in pieces(rows[0:1, :], 3)], axis=0).astype(BF16)
@@ -381,7 +402,7 @@
         parts = dot(readout_rows, act[c], NT) + dot(species_rows, centre)[:, 0:SLOTS]
         en_ref[c // 2, c % 2] = occupied_rows[c] * jnp.sum(parts, axis=0, keepdims=True)
     ones = jnp.ones((8, 128), F32)
-    own = [dot(ones, dacc[c], NT, lax.Precision.HIGHEST)[0:1, :] for c in range(4)]
+    own = [FORCE_SCALE * dot(ones, dacc[c], NT, lax.Precision.HIGHEST)[0:1, :] for c in range(4)]
     for copy in back_copies:
         copy.wait_recv()
     for c in range(4):
@@ -402,6 +423,14 @@
         copy.wait_send()
 
 
+def put_out(en_ref, fo_ref, en_out, fo_out, sems):
+    copies = [pltpu.make_async_copy(en_ref, en_out, sems.at[0]), pltpu.make_async_copy(fo_ref, fo_out, sems.at[1])]
+    for copy in copies:
+        copy.start()
+    for copy in copies:
+        copy.wait()
+
+
 def solution(mesh):
     sizes = tuple(mesh.shape[name] for name in ("gx", "gy", "gz"))
     in_specs = (
@@ -429,7 +458,7 @@
             w_energy.reshape(1, CH),
         )
         operands = [pltpu.with_memory_space_constraint(a, pltpu.HBM) for a in operands]
-        return pl.pallas_call(
+        results = pl.pallas_call(
             functools.partial(kernel, sizes),
             out_shape=(
                 jax.ShapeDtypeStruct(species.shape, F32),
@@ -464,6 +493,14 @@
                 collective_id=0, has_side_effects=True, vmem_limit_bytes=48 * 1024 * 1024
             ),
         )(*operands)
+        return pl.pallas_call(
+            put_out,
+            out_shape=tuple(jax.ShapeDtypeStruct(a.shape, a.dtype) for a in results),
+            in_specs=[anywhere] * 2,
+            out_specs=(anywhere, anywhere),
+            scratch_shapes=[pltpu.SemaphoreType.DMA((2,))],
+            compiler_params=pltpu.CompilerParams(vmem_limit_bytes=1024 * 1024),
+        )(*results)
 
     return jax.shard_map(
         on_device, mesh=mesh, in_specs=in_specs, out_specs=out_specs, check_vma=False

time: 41 us -> 40.2 us (0.980)
  local copies, waits for them, and re-layouts: 1.17 us -> 0 us
    unnamed x2 -> x0, local copies, waits for them, and re-layouts: 1.17 us -> none
    pallas_call x0 -> x1, Pallas kernels: none -> 0.62 us  [on_device(): pl.pallas_call(put_out, out_shape=tuple((jax.ShapeDtypeStruct(a.shape, a....]
where the time goes in v3:
time: 40.2 us; the launch traced here: 40 us
  Pallas kernels  39.4 us (98%)
  between operations  0.64 us (2%)
    pallas_call x1, Pallas kernels, on_device(): pl.pallas_call(functools.partial(kernel, sizes), out_shape=(jax.ShapeDtyp...  38.7 us

profile of v3, /device:TPU:1, one launch (start us, length us, event | category | flops | bytes accessed | tf_op | source)
XLA Modules:
  0.0 40.0 jit_solution(8462165597129558539)
XLA Ops:
  0.6 38.7 %shard_map.86 = (f32[2,2,1,64]{3,2,1,0:T(1,128)S(1)}, f32[2,2,1,192]{3,2,1,0:T(1,128)S(1)}) custom-call(f32[2,2,1,192]{3,2,1,0:T(1,128)} %pos_hbm.1, s32[2,2,1,64]{3,2,1,0:T(1,128)} %spec_hbm.1, s32[2,1,2]{2,1,0:T(1,128)} %bitcast.4, bf16[89,128]{1,0:T(8,128)(2,1)} %embed_hbm.1, bf16[128,512]{1,0:T(8,128)(2,1)} %filt_hbm.1, bf16[128,128]{1,0:T(8,128)(2,1)} %wup_hbm.1, ...), custom_call_target="tpu_custom_call" | custom-call | tf_op jit(solution)/shard_map/pallas_call | solution.py:461
  39.4 0.6 %shard_map.87 = (f32[2,2,1,64]{3,2,1,0:T(1,128)}, f32[2,2,1,192]{3,2,1,0:T(1,128)}) custom-call(f32[2,2,1,64]{3,2,1,0:T(1,128)S(1)} %get-tuple-element.4.en_ref, f32[2,2,1,192]{3,2,1,0:T(1,128)S(1)} %get-tuple-element.5.fo_ref), custom_call_target="tpu_custom_call" | custom-call | tf_op jit(solution)/shard_map/pallas_call | solution.py:496

commit v4 on v3

--- a/solution.py
+++ b/solution.py
@@ -58,12 +58,12 @@
 FAR_PAIRS = [
     ((FAR,) + a, (FAR,) + b)
     for a, b in (
-        ((0, 0), (1, 0)),
-        ((2, 0), (3, 0)),
+        ((0, 0), (3, 0)),
+        ((0, 3), (3, 3)),
+        ((1, 0), (2, 0)),
+        ((1, 3), (2, 3)),
+        ((0, 1), (0, 2)),
         ((3, 1), (3, 2)),
-        ((3, 3), (2, 3)),
-        ((1, 3), (0, 3)),
-        ((0, 2), (0, 1)),
         ((1, 1), (1, 2)),
         ((2, 1), (2, 2)),
     )
@@ -96,13 +96,23 @@
     return is_far(pair) and pair[0][1:] in OWN_COLUMNS
 
 
-def is_far_ring(pair):
-    return is_far(pair) and not is_far_core(pair)
-
-
-def corner_of(c):
-    cell = (FAR, 3 * (c // 2), 3 * (c % 2))
-    return next((t, pair.index(cell)) for t, pair in enumerate(PAIRS) if cell in pair)
+def is_far_corner(pair):
+    return is_far(pair) and all(part in (0, 3) for part in pair[0][1:])
+
+
+def is_far_side(pair):
+    return is_far(pair) and not is_far_core(pair) and not is_far_corner(pair)
+
+
+def rank(direction):
+    role, dx, dy = direction
+    if role == FAR:
+        return 2 + abs(dx) + abs(dy)
+    return 0 if direction == (NEAR, 0, 0) else 1
+
+
+def cells_in(directions):
+    return sum((2 - abs(dx)) * (2 - abs(dy)) for _, dx, dy in directions)
 
 
 def kernel(
@@ -212,8 +222,8 @@
         return pltpu.make_async_remote_copy(
             src_ref=pad.at[CENTRE, 1 + xs : 1 + xe, 1 + ys_ : 1 + ye],
             dst_ref=pad.at[role, tx:te, ty:tf],
-            send_sem=send1.at[n],
-            recv_sem=recv1.at[n],
+            send_sem=send1.at[0],
+            recv_sem=recv1.at[rank(DIRS[n])],
             device_id=device(role, dx, dy),
             device_id_type=MESH,
         )
@@ -295,18 +305,15 @@
                 place = slice(q * SLOTS + 8 * r, q * SLOTS + 8 * r + 8)
                 dacc[c, place, :] = own[q][r] if first else dacc[c, place, :] + own[q][r]
 
-    def give_back(t, halves=(0, 1)):
+    def give_back(t):
         low = lax.broadcasted_iota(jnp.int32, (1, 128), 1) < SLOTS
         fx, fy, fz = (-FORCE_SCALE * jnp.sum(racc[t, q], axis=0, keepdims=True) for q in range(3))
         swap = lambda v: pltpu.roll(v, SLOTS, 1)
-        for half in halves:
-            r, x, y = PAIRS[t][half]
-            if half:
-                back[r, x, y, 0:1, :] = jnp.where(low, swap(fx), fy)
-                back[r, x, y, 1:2, :] = jnp.where(low, swap(fz), 0.0)
-            else:
-                back[r, x, y, 0:1, :] = jnp.where(low, fx, swap(fy))
-                back[r, x, y, 1:2, :] = jnp.where(low, fz, 0.0)
+        (ra, xa, ya), (rb, xb, yb) = PAIRS[t]
+        back[ra, xa, ya, 0:1, :] = jnp.where(low, fx, swap(fy))
+        back[ra, xa, ya, 1:2, :] = jnp.where(low, fz, 0.0)
+        back[rb, xb, yb, 0:1, :] = jnp.where(low, swap(fx), fy)
+        back[rb, xb, yb, 1:2, :] = jnp.where(low, swap(fz), 0.0)
 
     def collect(n):
         role, dx, dy = DIRS[n]
@@ -314,18 +321,20 @@
         return pltpu.make_async_remote_copy(
             src_ref=back.at[role, xs:xe, ys_:ye],
             dst_ref=rec.at[n, 0 : xe - xs, 0 : ye - ys_],
-            send_sem=send2.at[n],
-            recv_sem=recv2.at[n],
+            send_sem=send2.at[0],
+            recv_sem=recv2.at[0],
             device_id=device(role, dx, dy),
             device_id_type=MESH,
         )
 
     racc[...] = jnp.zeros_like(racc)
 
-    def arrive(wanted):
-        for n, d in enumerate(DIRS):
-            if wanted(d):
-                out_copies[n].wait_recv()
+    def finish(semaphore, directions):
+        shape_of = rec.at[0 : cells_in(directions) // 4]
+        pltpu.make_async_copy(shape_of, shape_of, semaphore).wait()
+
+    def arrive(order):
+        finish(recv1.at[order], [d for d in DIRS if rank(d) == order])
 
     def take_in(wanted, first=False):
         for t, pair in enumerate(PAIRS):
@@ -335,14 +344,16 @@
             part = weight_sums(c, tiles_of(c, wanted))
             sbuf[c] = part if first else sbuf[c] + part
 
-    arrive(lambda d: d == (NEAR, 0, 0))
+    arrive(0)
     take_in(is_own, True)
-    arrive(lambda d: d[0] != FAR and d != (NEAR, 0, 0))
+    arrive(1)
     take_in(is_side)
-    arrive(lambda d: d == (FAR, 0, 0))
+    arrive(2)
     take_in(is_far_core)
-    arrive(lambda d: d[0] == FAR and d[1:] != (0, 0))
-    take_in(is_far_ring)
+    arrive(3)
+    take_in(is_far_side)
+    arrive(4)
+    take_in(is_far_corner)
 
     slot_row = lax.broadcasted_iota(jnp.int32, (SLOTS, CH), 0)
     split = []
@@ -366,33 +377,21 @@
         abuf[c] = jnp.concatenate(pieces(mine, 2), axis=1)
     back_copies = [collect(n) for n in range(len(DIRS))]
 
-    def send_back(wanted):
-        for n, d in enumerate(DIRS):
-            if wanted(d):
-                back_copies[n].start()
-
-    corners = [corner_of(c) for c in range(4)]
-    for c in range(4):
-        pair_forces(c, [corners[c][0]], True)
-    for t, half in corners:
-        give_back(t, (half,))
-    send_back(lambda d: d[0] == FAR and 0 not in d[1:])
-
-    def react(wanted):
+    def react(wanted, sends, first=False):
         for c in range(4):
-            pair_forces(c, [t for t in tiles_of(c, wanted) if t != corners[c][0]], False)
+            pair_forces(c, tiles_of(c, wanted), first)
         for t, pair in enumerate(PAIRS):
             if wanted(pair):
-                give_back(t, [h for h in (0, 1) if (t, h) not in corners])
-
-    react(is_far_ring)
-    send_back(lambda d: d[0] == FAR and d[1:].count(0) == 1)
-    react(is_side)
-    send_back(lambda d: d[0] != FAR and d[1:] != (0, 0))
-    react(is_far_core)
-    send_back(lambda d: d == (FAR, 0, 0))
-    react(is_own)
-    send_back(lambda d: d == (NEAR, 0, 0))
+                give_back(t)
+        for n, d in enumerate(DIRS):
+            if sends(d):
+                back_copies[n].start()
+
+    react(is_far_corner, lambda d: rank(d) == 4, True)
+    react(is_far_side, lambda d: rank(d) == 3)
+    react(is_side, lambda d: rank(d) == 1)
+    react(is_far_core, lambda d: rank(d) == 2)
+    react(is_own, lambda d: rank(d) == 0)
 
     occupied_rows = [(slot_lane < counts[c]).astype(F32) for c in range(4)]
     readout_rows = jnp.concatenate([p.astype(F32) for p in pieces(rows[0:1, :], 3)], axis=0).astype(BF16)
@@ -403,8 +402,7 @@
         en_ref[c // 2, c % 2] = occupied_rows[c] * jnp.sum(parts, axis=0, keepdims=True)
     ones = jnp.ones((8, 128), F32)
     own = [FORCE_SCALE * dot(ones, dacc[c], NT, lax.Precision.HIGHEST)[0:1, :] for c in range(4)]
-    for copy in back_copies:
-        copy.wait_recv()
+    finish(recv2.at[0], DIRS)
     for c in range(4):
         x, y = c // 2, c % 2
         total = back[CENTRE, 1 + x, 1 + y]
@@ -417,10 +415,8 @@
         mask = occupied_rows[c]
         fo_ref[c // 2, c % 2, :, 0:128] = planar * jnp.concatenate([mask, mask], axis=1)
         fo_ref[c // 2, c % 2, :, 128:192] = upright * mask
-    for copy in out_copies:
-        copy.wait_send()
-    for copy in back_copies:
-        copy.wait_send()
+    finish(send1.at[0], DIRS)
+    finish(send2.at[0], DIRS)
 
 
 def put_out(en_ref, fo_ref, en_out, fo_out, sems):
@@ -484,10 +480,10 @@
                 pltpu.VMEM((4, SLOTS, CH), BF16),
                 pltpu.VMEM((24, 3, 8, 128), F32),
                 pltpu.VMEM((4, 3 * SLOTS, 128), F32),
-                pltpu.SemaphoreType.DMA((count,)),
-                pltpu.SemaphoreType.DMA((count,)),
-                pltpu.SemaphoreType.DMA((count,)),
-                pltpu.SemaphoreType.DMA((count,)),
+                pltpu.SemaphoreType.DMA((1,)),
+                pltpu.SemaphoreType.DMA((5,)),
+                pltpu.SemaphoreType.DMA((1,)),
+                pltpu.SemaphoreType.DMA((1,)),
             ],
             compiler_params=pltpu.CompilerParams(
                 collective_id=0, has_side_effects=True, vmem_limit_bytes=48 * 1024 * 1024

time: 40.2 us -> 39.4 us (0.980)
  Pallas kernels: 39.4 us -> 38.6 us
    pallas_call x1, Pallas kernels: 38.7 us -> 38 us  [on_device(): pl.pallas_call(functools.partial(kernel, sizes), out_shape=(jax.ShapeDtyp...]
where the time goes in v4:
time: 39.4 us; the launch traced here: 39.2 us
  Pallas kernels  38.6 us (98%)
  between operations  0.64 us (2%)
    pallas_call x1, Pallas kernels, on_device(): pl.pallas_call(functools.partial(kernel, sizes), out_shape=(jax.ShapeDtyp...  38 us

profile of v4, /device:TPU:1, one launch (start us, length us, event | category | flops | bytes accessed | tf_op | source)
XLA Modules:
  0.0 39.2 jit_solution(7283767133485150545)
XLA Ops:
  0.6 38.0 %shard_map.86 = (f32[2,2,1,64]{3,2,1,0:T(1,128)S(1)}, f32[2,2,1,192]{3,2,1,0:T(1,128)S(1)}) custom-call(f32[2,2,1,192]{3,2,1,0:T(1,128)} %pos_hbm.1, s32[2,2,1,64]{3,2,1,0:T(1,128)} %spec_hbm.1, s32[2,1,2]{2,1,0:T(1,128)} %bitcast.4, bf16[89,128]{1,0:T(8,128)(2,1)} %embed_hbm.1, bf16[128,512]{1,0:T(8,128)(2,1)} %filt_hbm.1, bf16[128,128]{1,0:T(8,128)(2,1)} %wup_hbm.1, ...), custom_call_target="tpu_custom_call" | custom-call | tf_op jit(solution)/shard_map/pallas_call | solution.py:457
  38.6 0.6 %shard_map.87 = (f32[2,2,1,64]{3,2,1,0:T(1,128)}, f32[2,2,1,192]{3,2,1,0:T(1,128)}) custom-call(f32[2,2,1,64]{3,2,1,0:T(1,128)S(1)} %get-tuple-element.4.en_ref, f32[2,2,1,192]{3,2,1,0:T(1,128)S(1)} %get-tuple-element.5.fo_ref), custom_call_target="tpu_custom_call" | custom-call | tf_op jit(solution)/shard_map/pallas_call | solution.py:492

commit v5 on v4

--- a/solution.py
+++ b/solution.py
@@ -149,6 +149,7 @@
     act,
     racc,
     dacc,
+    geo,
     send1,
     recv1,
     send2,
@@ -260,12 +261,18 @@
         decaying = [jnp.exp2((-0.5 * LOG2E * 3.0**k / HALF**2) * dist_sq) for k in range(RAD)]
         return dx, dy, dz, falloff, decaying
 
+    def keeps(t):
+        return True
+
     def weight_sums(c, tiles):
         columns = []
         for t in tiles:
             blocks = [[] for _ in range(RAD)]
             for lo in range(0, SLOTS, 16):
-                _, _, _, falloff, decaying = geometry(c, t, lo, 16)
+                dx, dy, dz, falloff, decaying = geometry(c, t, lo, 16)
+                if keeps(t):
+                    for m, values in enumerate((dx, dy, dz, falloff, *decaying)):
+                        geo[c, t, m, lo : lo + 16, :] = values
                 square = falloff * falloff
                 if t == (1 + c // 2) * 4 + 1 + c % 2:
                     i = lax.broadcasted_iota(jnp.int32, (16, 128), 0) + lo
@@ -286,7 +293,10 @@
             for n, t in enumerate(group):
                 other = [None] * 3
                 for r in range(SLOTS // 8):
-                    dx, dy, dz, falloff, decaying = geometry(c, t, 8 * r, 8)
+                    if keeps(t):
+                        dx, dy, dz, falloff, *decaying = (geo[c, t, m, 8 * r : 8 * r + 8, :] for m in range(8))
+                    else:
+                        dx, dy, dz, falloff, decaying = geometry(c, t, 8 * r, 8)
                     q0, q1, q2, q3 = (
                         e * gathered[k * SLOTS + 8 * r : k * SLOTS + 8 * r + 8, n * 128 : (n + 1) * 128]
                         for k, e in enumerate(decaying)
@@ -480,6 +490,7 @@
                 pltpu.VMEM((4, SLOTS, CH), BF16),
                 pltpu.VMEM((24, 3, 8, 128), F32),
                 pltpu.VMEM((4, 3 * SLOTS, 128), F32),
+                pltpu.VMEM((4, len(PAIRS), 8, SLOTS, 128), F32),
                 pltpu.SemaphoreType.DMA((1,)),
                 pltpu.SemaphoreType.DMA((5,)),
                 pltpu.SemaphoreType.DMA((1,)),

time: 39.4 us -> 39.4 us (level)
  no operation moved by 1% of the time
where the time goes in v5:
time: 39.4 us; the launch traced here: 39.3 us
  Pallas kernels  38.6 us (98%)
  between operations  0.64 us (2%)
    pallas_call x1, Pallas kernels, on_device(): pl.pallas_call(functools.partial(kernel, sizes), out_shape=(jax.ShapeDtyp...  38 us

profile of v5, /device:TPU:1, one launch (start us, length us, event | category | flops | bytes accessed | tf_op | source)
XLA Modules:
  0.0 39.3 jit_solution(17292392734762667714)
XLA Ops:
  0.6 38.0 %shard_map.86 = (f32[2,2,1,64]{3,2,1,0:T(1,128)S(1)}, f32[2,2,1,192]{3,2,1,0:T(1,128)S(1)}) custom-call(f32[2,2,1,192]{3,2,1,0:T(1,128)} %pos_hbm.1, s32[2,2,1,64]{3,2,1,0:T(1,128)} %spec_hbm.1, s32[2,1,2]{2,1,0:T(1,128)} %bitcast.4, bf16[89,128]{1,0:T(8,128)(2,1)} %embed_hbm.1, bf16[128,512]{1,0:T(8,128)(2,1)} %filt_hbm.1, bf16[128,128]{1,0:T(8,128)(2,1)} %wup_hbm.1, ...), custom_call_target="tpu_custom_call" | custom-call | tf_op jit(solution)/shard_map/pallas_call | solution.py:467
  38.7 0.6 %shard_map.87 = (f32[2,2,1,64]{3,2,1,0:T(1,128)}, f32[2,2,1,192]{3,2,1,0:T(1,128)}) custom-call(f32[2,2,1,64]{3,2,1,0:T(1,128)S(1)} %get-tuple-element.4.en_ref, f32[2,2,1,192]{3,2,1,0:T(1,128)S(1)} %get-tuple-element.5.fo_ref), custom_call_target="tpu_custom_call" | custom-call | tf_op jit(solution)/shard_map/pallas_call | solution.py:503
